TPU v7x, 512 devices: a whole 4x8x8 slice. The times are simulated.
512 devices in a mesh: seq: 64 (over z_hi, y, core), tp: 8 (over x, z_lo).
Axes of the slice: x: 4, y: 8, z: 8 (z_hi: 4, z_lo: 2; z = z_hi * 2 + z_lo), core: 2. Of those that a mesh axis runs over, the one named last changes fastest.
Arguments:
- prompt_states: bfloat16 [2, 64, 64, 2048], P(None, 'seq', None, 'tp'), may hold values from -8 to 8
- cont_states: bfloat16 [2, 64, 8, 2048], P(None, 'seq', None, 'tp'), may hold values from -8 to 8
- cache_kv: bfloat16 [2, 64, 448, 2048], P(None, 'seq', None, 'tp'), may hold values from -5 to 5
- cache_lengths: int32 [64], replicated, may hold values from 1 to 448, 14336 in all
- w_query: bfloat16 [2048, 2048], P(None, 'tp'), may hold values from -2 to 2
- w_key: bfloat16 [2048, 2048], P(None, 'tp'), may hold values from -2 to 2
- w_value: bfloat16 [2048, 2048], P(None, 'tp'), may hold values from -0.125 to 0.125
- w_out: bfloat16 [2048, 2048], P('tp'), may hold values from -2 to 2
- q_gain: float32 [2048], P('tp'), may hold values from 0 to 10
- k_gain: float32 [2048], P('tp'), may hold values from 0 to 10
- post_gain: float32 [2048], P('tp'), may hold values from 0.5 to 1.5
Outputs:
- hidden_prompt: bfloat16 [2, 64, 64, 2048], P(None, 'seq', None, 'tp')
- hidden_cont: bfloat16 [2, 64, 8, 2048], P(None, 'seq', None, 'tp')
- kv_cache: bfloat16 [2, 64, 128, 2048], P(None, 'seq', None, 'tp')
Inputs may be any that keep to these rules, and one draw needn't show every extreme that they name: The cache_lengths[d] live slots of seq index d are its first ones; the lengths sum to 14336 and the largest equals 448.
All inputs are finite; a program needn't handle non-finite values.
Results may differ from a plain program's by a relative error of at most 0.029.
Values may be sent and summed in bfloat16 or wider, within the bound.
A program may use at most 64 MiB of HBM per device.

v0:
```python
import jax
import jax.numpy as jnp
from jax import lax
from jax.sharding import PartitionSpec as P

HD = 128


EPS = 1e-06
THETA = 500000.0
NEG = -1e30


def rotate(field, positions):
    half_dim = field.shape[-1] // 2
    inverse = THETA ** (-(jnp.arange(half_dim, dtype=jnp.float32) * 2.0 / field.shape[-1]))
    angles = positions.astype(jnp.float32)[:, None] * inverse[None, :]
    cosine = jnp.cos(angles)[:, None, :]
    sine_part = jnp.sin(angles)[:, None, :]
    front_half = field[..., :half_dim]
    back_half = field[..., half_dim:]
    return jnp.concatenate(
        [front_half * cosine - back_half * sine_part, back_half * cosine + front_half * sine_part],
        -1,
    )


def absorb(state, queries, keys, values, allowed):
    running_max, running_sum, running_out = state
    scores = jnp.einsum(
        "rhd,khd->hrk", queries, keys, preferred_element_type=jnp.float32
    ) * queries.shape[-1] ** (-0.5)
    scores = jnp.where(allowed[None], scores, NEG)
    new_max = jnp.maximum(running_max, jnp.max(scores, -1))
    weights = jnp.where(allowed[None], jnp.exp(scores - new_max[..., None]), 0.0)
    shrink = jnp.exp(running_max - new_max)
    running_sum = running_sum * shrink + jnp.sum(weights, -1)
    summed = jnp.einsum(
        "hrk,khd->hrd", weights.astype(jnp.bfloat16), values, preferred_element_type=jnp.float32
    )
    running_out = running_out * shrink[..., None] + summed
    return (new_max, running_sum, running_out)


def empty_state(head_count, row_count, head_dim):
    return (
        jnp.full((head_count, row_count), NEG, jnp.float32),
        jnp.zeros((head_count, row_count), jnp.float32),
        jnp.zeros((head_count, row_count, head_dim), jnp.float32),
    )


def per_device(
    prompt_states,
    cont_states,
    cache_kv,
    cache_lengths,
    w_query,
    w_key,
    w_value,
    w_out,
    q_gain,
    k_gain,
    post_gain,
):
    seq_count = lax.axis_size("seq")
    tp_count = lax.axis_size("tp")
    seq_index = lax.axis_index("seq")
    block_len = prompt_states.shape[2]
    cont_len = cont_states.shape[2]
    capacity = cache_kv.shape[2]
    local_width = w_query.shape[1]
    head_count = local_width // HD
    prompt_rows = 2 * block_len
    cont_rows = 2 * cont_len
    cached = seq_count * capacity // 2
    full_prompt, full_cont = (
        lax.all_gather(prompt_states, "tp", axis=3, tiled=True),
        lax.all_gather(cont_states, "tp", axis=3, tiled=True),
    )
    model_width = full_prompt.shape[3]
    all_rows = jnp.concatenate(
        [full_prompt.reshape(prompt_rows, model_width), full_cont.reshape(cont_rows, model_width)],
        0,
    )
    query_proj = jnp.dot(all_rows, w_query, preferred_element_type=jnp.float32)
    key_proj = jnp.dot(all_rows, w_key, preferred_element_type=jnp.float32)
    value_proj = jnp.dot(all_rows, w_value, preferred_element_type=jnp.float32)
    query_sq, key_sq = lax.psum(
        (jnp.sum(query_proj * query_proj, -1), jnp.sum(key_proj * key_proj, -1)), "tp"
    )
    total_width = local_width * tp_count
    query_norm = query_proj * lax.rsqrt(query_sq / total_width + EPS)[:, None] * q_gain[None, :]
    key_norm = key_proj * lax.rsqrt(key_sq / total_width + EPS)[:, None] * k_gain[None, :]

    def device_positions(first_device, device_count, length, offset):
        devices = first_device + jnp.arange(device_count, dtype=jnp.int32)
        blocks = jnp.stack([devices, 2 * seq_count - 1 - devices], 1)
        return (
            offset
            + blocks[:, :, None] * length
            + jnp.arange(length, dtype=jnp.int32)[None, None, :]
        ).reshape(-1)

    prompt_pos = device_positions(seq_index, 1, block_len, 0)
    cont_pos = device_positions(seq_index, 1, cont_len, cached)
    positions = jnp.concatenate([prompt_pos, cont_pos])
    queries = rotate(query_norm.reshape(-1, head_count, HD), positions).astype(jnp.bfloat16)
    keys = rotate(key_norm.reshape(-1, head_count, HD), positions).astype(jnp.bfloat16)
    values = value_proj.astype(jnp.bfloat16).reshape(-1, head_count, HD)
    query_prompt = queries[:prompt_rows]
    query_cont = queries[prompt_rows:]
    key_prompt = keys[:prompt_rows]
    key_cont = keys[prompt_rows:]
    value_prompt = values[:prompt_rows]
    value_cont = values[prompt_rows:]
    cache_keys = cache_kv[0, 0].reshape(capacity, head_count, HD)
    cache_values = cache_kv[1, 0].reshape(capacity, head_count, HD)
    live_count = cache_lengths[seq_index]
    live_slots = (jnp.arange(capacity, dtype=jnp.int32) < live_count)[None, :]
    prompt_init = empty_state(head_count, prompt_rows, HD)
    all_queries = lax.all_gather(query_cont[None], "seq", axis=0, tiled=True)
    query_rows = all_queries.reshape(-1, head_count, HD)
    state = empty_state(head_count, query_rows.shape[0], HD)
    state = absorb(state, query_rows, cache_keys, cache_values, live_slots)
    cont_state = absorb(
        state,
        query_rows,
        key_cont,
        value_cont,
        cont_pos[None, :] <= device_positions(0, seq_count, cont_len, cached)[:, None],
    )
    key_piece = lax.all_gather(key_prompt[None], "seq", axis=0, tiled=True)
    key_pos = device_positions(jnp.int32(0), key_piece.shape[0], block_len, 0)
    allowed = key_pos[None, :] <= prompt_pos[:, None]
    prompt_state = absorb(
        prompt_init,
        query_prompt,
        key_piece.reshape(-1, head_count, HD),
        lax.all_gather(value_prompt[None], "seq", axis=0, tiled=True).reshape(-1, head_count, HD),
        allowed,
    )
    cont_max, cont_sum, cont_out = cont_state
    recv_max, recv_sum, recv_out = (
        lax.all_to_all(
            cont_max.reshape(head_count, seq_count, cont_rows),
            "seq",
            split_axis=1,
            concat_axis=1,
            tiled=True,
        ),
        lax.all_to_all(
            cont_sum.reshape(head_count, seq_count, cont_rows),
            "seq",
            split_axis=1,
            concat_axis=1,
            tiled=True,
        ),
        lax.all_to_all(
            cont_out.reshape(head_count, seq_count, cont_rows, HD),
            "seq",
            split_axis=1,
            concat_axis=1,
            tiled=True,
        ),
    )
    global_max = jnp.max(recv_max, 1, keepdims=True)
    rescale = jnp.exp(recv_max - global_max)
    numerator = jnp.sum(recv_out * rescale[..., None], 1)
    denominator = jnp.sum(recv_sum * rescale, 1)
    cont_attended = numerator / denominator[..., None]
    prompt_attended = prompt_state[2] / prompt_state[1][..., None]
    attended = (
        jnp.concatenate([prompt_attended, cont_attended], 1)
        .transpose(1, 0, 2)
        .reshape(-1, local_width)
        .astype(jnp.bfloat16)
    )
    partial_value = jnp.dot(attended, w_out, preferred_element_type=jnp.float32)
    projected = lax.psum_scatter(
        partial_value.astype(jnp.bfloat16), "tp", scatter_dimension=1, tiled=True
    ).astype(jnp.float32)
    proj_sq = lax.psum(jnp.sum(projected * projected, -1), "tp")
    normed = projected * lax.rsqrt(proj_sq / model_width + EPS)[:, None] * post_gain[None, :]
    local_rows = jnp.concatenate(
        [prompt_states.reshape(prompt_rows, -1), cont_states.reshape(cont_rows, -1)], 0
    ).astype(jnp.float32)
    hidden = (local_rows + normed).astype(jnp.bfloat16)
    hidden_prompt = hidden[:prompt_rows].reshape(2, 1, block_len, -1)
    hidden_cont = hidden[prompt_rows:].reshape(2, 1, cont_len, -1)
    rounds = block_len // seq_count

    def to_cyclic(field):
        return field.reshape(2, rounds, seq_count, local_width).transpose(0, 2, 1, 3)

    def from_cyclic(field):
        return jnp.concatenate(
            [
                field[0].reshape(block_len, local_width),
                field[1][::-1].reshape(block_len, local_width),
            ],
            0,
        )

    recv_keys, recv_values = (
        lax.all_to_all(to_cyclic(key_prompt), "seq", split_axis=1, concat_axis=1, tiled=True),
        lax.all_to_all(to_cyclic(value_prompt), "seq", split_axis=1, concat_axis=1, tiled=True),
    )
    kv_cache = jnp.stack([from_cyclic(recv_keys), from_cyclic(recv_values)])[:, None]
    return (hidden_prompt, hidden_cont, kv_cache)


def solution(mesh):
    return jax.shard_map(
        per_device,
        mesh=mesh,
        in_specs=(
            P(None, "seq", None, "tp"),
            P(None, "seq", None, "tp"),
            P(None, "seq", None, "tp"),
            P(),
            P(None, "tp"),
            P(None, "tp"),
            P(None, "tp"),
            P("tp", None),
            P("tp"),
            P("tp"),
            P("tp"),
        ),
        out_specs=(
            P(None, "seq", None, "tp"),
            P(None, "seq", None, "tp"),
            P(None, "seq", None, "tp"),
        ),
        check_vma=False,
    )
```

profile of v0, /device:TPU:1, one launch (start us, length us, event | category | flops | bytes accessed | tf_op | source)
XLA Modules:
  0.0 360.9 jit_solution(1940120923736906404)
XLA Ops:
  7.8 23.7 %all_gather.16 = bf16[2,1,8,2048]{3,2,1,0:T(8,128)(2,1)S(1)} all-gather(bf16[2,1,8,256]{3,2,1,0:T(8,128)(2,1)} %param.12), channel_id=1, replica_groups=mesh['seq'=64,'tp'=8] {'tp'}, dimensions={3}, use_global_device_ids=true | all-gather | bytes 73728 | tf_op jit(solution)/shard_map/all_gather | solution.py:79
  31.5 24.9 %all_gather.15 = bf16[2,1,64,2048]{3,2,1,0:T(8,128)(2,1)S(1)} all-gather(bf16[2,1,64,256]{3,2,1,0:T(8,128)(2,1)} %param.11), channel_id=1, replica_groups=mesh['seq'=64,'tp'=8] {'tp'}, dimensions={3}, use_global_device_ids=true | all-gather | bytes 589824 | tf_op jit(solution)/shard_map/all_gather | solution.py:78
  56.4 1.7 multiply_reduce_fusion.1
  58.1 1.7 multiply_reduce_fusion.2
  59.8 15.1 %all-reduce = (f32[144]{0:T(256)S(1)}, f32[144]{0:T(256)S(1)}) all-reduce(f32[144]{0:T(256)S(1)} %get-tuple-element.50, f32[144]{0:T(256)S(1)} %get-tuple-element.52), channel_id=1, replica_groups=mesh['seq'=64,'tp'=8] {'tp'}, use_global_device_ids=true, to_apply=%region_1.0 | all-reduce | flops 288 | bytes 2304 | tf_op jit(solution)/shard_map/psum | solution.py:89
  75.2 0.2 fusion.67
  75.4 0.2 fusion.66
  75.7 0.5 copy-done.11
  76.2 0.3 multiply_cosine_fusion
  76.7 0.7 fusion.43
  77.4 1.6 convolution_convert_fusion.1
  79.1 0.6 copy.92
  79.7 0.6 broadcast_multiply_fusion
  80.3 0.1 copy.96
  80.4 0.1 iota_add_fusion
  80.6 0.1 add.198
  80.7 1.1 fusion.65
  82.0 106.0 %all-gather.1 = bf16[1024,2,128]{2,0,1:T(8,128)(2,1)S(1)} all-gather(bf16[16,2,128]{2,0,1:T(8,128)(2,1)S(1)} %pad_maximum_fusion.6), channel_id=3, replica_groups=mesh['seq'=64,'tp'=8] {'seq'}, dimensions={0}, use_global_device_ids=true | all-gather | bytes 532480 | tf_op jit(solution)/shard_map/all_gather | solution.py:122
  188.0 0.3 fusion.70
  188.4 0.6 dynamic_slice.3
  189.0 0.6 iota_compare_fusion
  189.7 2.5 fusion.8
  192.3 3.1 fusion.9
  195.7 0.7 copy.100
  196.4 4.2 %all-to-all-start.2 = ((f32[2,64,16]{2,0,1:T(2,128)}), f32[2,64,16]{2,0,1:T(2,128)S(1)}, u32[]{:S(2)}, u32[]{:S(2)}) async-start(f32[2,64,16]{2,0,1:T(2,128)} %copy.100), calls=%async_computation.2 | async-start | bytes 131072 | tf_op jit(solution)/shard_map/all_to_all | solution.py:152
  200.7 3.4 fusion.17
  204.1 0.7 copy.99
  204.8 8.3 %all-to-all-done.2 = f32[2,64,16]{2,0,1:T(2,128)S(1)} async-done(((f32[2,64,16]{2,0,1:T(2,128)}), f32[2,64,16]{2,0,1:T(2,128)S(1)}, u32[]{:S(2)}, u32[]{:S(2)}) %all-to-all-start.2) | async-done | bytes 8224 | tf_op jit(solution)/shard_map/all_to_all | solution.py:152
  213.1 0.6 copy-done.6
  213.7 4.5 %all-to-all-start.1 = ((f32[2,64,16]{2,0,1:T(2,128)}), f32[2,64,16]{2,0,1:T(2,128)S(1)}, u32[]{:S(2)}, u32[]{:S(2)}) async-start(f32[2,64,16]{2,0,1:T(2,128)} %copy.99), calls=%async_computation.1 | async-start | bytes 131072 | tf_op jit(solution)/shard_map/all_to_all | solution.py:145
  218.2 1.1 convolution_add_fusion
  219.4 1.4 copy.87
  220.8 1.1 copy.98
  221.9 8.5 %all-to-all-done.1 = f32[2,64,16]{2,0,1:T(2,128)S(1)} async-done(((f32[2,64,16]{2,0,1:T(2,128)}), f32[2,64,16]{2,0,1:T(2,128)S(1)}, u32[]{:S(2)}, u32[]{:S(2)}) %all-to-all-start.1) | async-done | bytes 8224 | tf_op jit(solution)/shard_map/all_to_all | solution.py:145
  230.4 4.5 %all-to-all-start = ((f32[2,64,16,128]{3,2,0,1:T(8,128)}), f32[2,64,16,128]{3,2,0,1:T(8,128)S(1)}, u32[]{:S(2)}, u32[]{:S(2)}) async-start(f32[2,64,16,128]{3,2,0,1:T(8,128)} %copy.98), calls=%async_computation | async-start | bytes 2097152 | tf_op jit(solution)/shard_map/all_to_all | solution.py:159
  234.9 0.2 reduce-scatter.2.cloned.1.call-start
  235.1 0.9 iota_add_fusion.1
  236.0 0.7 add.172
  236.7 1.4 broadcast_compare_fusion
  238.1 0.6 reduce_max.42
  238.8 1.3 multiply_reduce_fusion.3
  240.1 26.2 %all-to-all-done = f32[2,64,16,128]{3,2,0,1:T(8,128)S(1)} async-done(((f32[2,64,16,128]{3,2,0,1:T(8,128)}), f32[2,64,16,128]{3,2,0,1:T(8,128)S(1)}, u32[]{:S(2)}, u32[]{:S(2)}) %all-to-all-start) | async-done | bytes 1048608 | tf_op jit(solution)/shard_map/all_to_all | solution.py:159
  266.3 0.3 multiply_reduce_fusion
  266.6 0.8 divide_convert_fusion
  267.4 4.5 %fusion.71 = (f32[2,128]{1,0:T(2,128)S(1)}, f32[2,128,8192]{2,1,0:T(8,128)S(1)}) fusion(bf16[8192,2,128]{2,0,1:T(8,128)(2,1)} %all-gather.7.cloned.1.call-done, bf16[144,2,64]{2,0,1:T(8,128)(2,1)S(1)} %get-tuple-element.31, bf16[144,2,64]{2,0,1:T(8,128)(2,1)S(1)} %get-tuple-element.30, pred[128,8192]{1,0:T(8,128)(4,1)S(1)} %broadcast_compare_fusion), kind=kOutput, calls=%fused_computation.122 | convolution fusion | flops 543293184 | bytes 13706240 | tf_op jit(solution)/shard_map/rhd,khd->hrk/dot_general | solution.py:30
  271.9 2.1 fusion.1
  274.1 1.1 copy-done.1
  275.2 15.5 %all-gather.5.cloned.1.call-done = bf16[64,128,2,128]{3,1,2,0:T(8,128)(2,1)} async-done(((bf16[1,128,2,128]{3,1,2,0:T(8,128)(2,1)}), bf16[64,128,2,128]{3,1,2,0:T(8,128)(2,1)}) %all-gather.5.cloned.1.call-update) | async-done | bytes 4194320 | tf_op jit(solution)/shard_map/all_gather | solution.py:140
  290.7 2.8 copy.93
  293.6 1.8 copy-done.2
  295.4 2.3 fusion.27
  297.7 1.1 convolution_convert_fusion
  298.9 0.7 copy.106
  299.6 7.2 %all-to-all-start.4 = ((bf16[2,64,1,256]{3,0,2,1:T(2,128)(2,1)}), bf16[2,64,1,256]{3,0,2,1:T(2,128)(2,1)S(1)}, u32[]{:S(2)}, u32[]{:S(2)}) async-start(bf16[2,64,1,256]{3,0,2,1:T(2,128)(2,1)} %copy.106), calls=%async_computation.5 | async-start | bytes 131072 | tf_op jit(solution)/shard_map/all_to_all | solution.py:207
  307.0 0.7 copy.103
  307.7 11.4 %all-to-all-done.4 = bf16[2,64,1,256]{3,0,2,1:T(2,128)(2,1)S(1)} async-done(((bf16[2,64,1,256]{3,0,2,1:T(2,128)(2,1)}), bf16[2,64,1,256]{3,0,2,1:T(2,128)(2,1)S(1)}, u32[]{:S(2)}, u32[]{:S(2)}) %all-to-all-start.4) | async-done | bytes 65568 | tf_op jit(solution)/shard_map/all_to_all | solution.py:207
  319.0 4.4 %all-to-all-start.3 = ((bf16[2,64,1,256]{3,0,2,1:T(2,128)(2,1)}), bf16[2,64,1,256]{3,0,2,1:T(2,128)(2,1)S(1)}, u32[]{:S(2)}, u32[]{:S(2)}) async-start(bf16[2,64,1,256]{3,0,2,1:T(2,128)(2,1)} %copy.103), calls=%async_computation.4 | async-start | bytes 131072 | tf_op jit(solution)/shard_map/all_to_all | solution.py:206
  323.7 12.1 %all-to-all-done.3 = bf16[2,64,1,256]{3,0,2,1:T(2,128)(2,1)S(1)} async-done(((bf16[2,64,1,256]{3,0,2,1:T(2,128)(2,1)}), bf16[2,64,1,256]{3,0,2,1:T(2,128)(2,1)S(1)}, u32[]{:S(2)}, u32[]{:S(2)}) %all-to-all-start.3) | async-done | bytes 65568 | tf_op jit(solution)/shard_map/all_to_all | solution.py:206
  336.0 0.7 maximum_bitcast_fusion
  336.7 1.0 fusion.35
  337.7 14.4 %psum.23 = f32[144]{0:T(256)S(1)} all-reduce(f32[144]{0:T(256)S(1)} %fusion.35), channel_id=1, replica_groups=mesh['seq'=64,'tp'=8] {'tp'}, use_global_device_ids=true, to_apply=%region_15.16 | all-reduce | flops 144 | bytes 1152 | tf_op jit(solution)/shard_map/psum | solution.py:183
  352.2 1.0 fusion.38
  353.2 0.6 slice_bitcast_fusion
  353.8 0.6 slice.87
  (86 shorter events, 2.5 us)
Async XLA Ops:
  7.2 290.5 %copy-start = (bf16[256,2048]{1,0:T(8,128)(2,1)S(1)}, bf16[256,2048]{1,0:T(8,128)(2,1)}, u32[]{:S(2)}) copy-start(bf16[256,2048]{1,0:T(8,128)(2,1)} %param.18) | copy-start | bytes 3145732
  7.2 67.7 %copy-start.13 = (f32[256]{0:T(256)S(1)}, f32[256]{0:T(256)}, u32[]{:S(2)}) copy-start(f32[256]{0:T(256)} %param.20) | copy-start | bytes 3076
  7.2 67.8 %copy-start.14 = (f32[256]{0:T(256)S(1)}, f32[256]{0:T(256)}, u32[]{:S(2)}) copy-start(f32[256]{0:T(256)} %param.19) | copy-start | bytes 3076
  7.2 260.2 %all-gather.7.cloned.1.call-start = ((), (), s32[]{:S(2)}) async-start(), calls=%async_computation.8 | async-start | bytes 4259840 | tf_op jit(solution)/shard_map/all_gather | solution.py:133
  75.7 112.8 %copy-start.16 = (s32[64]{0:T(128)S(1)}, s32[64]{0:T(128)}, u32[]{:S(2)}) copy-start(s32[64]{0:T(128)} %param.14) | copy-start | bytes 772
  75.7 0.5 copy-start.11
  77.4 213.3 %all-gather.5.cloned.1.call-start = ((), (), s32[]{:S(2)}) async-start(), calls=%async_computation.6 | async-start | bytes 4259840 | tf_op jit(solution)/shard_map/all_gather | solution.py:140
  79.0 113.2 %copy-start.9 = (bf16[144,256]{1,0:T(8,128)(2,1)}, bf16[144,256]{1,0:T(8,128)(2,1)S(1)}, u32[]{:S(2)}) copy-start(bf16[144,256]{1,0:T(8,128)(2,1)S(1)} %convolution_convert_fusion.1) | copy-start | bytes 221188
  82.0 113.5 %copy-start.4 = (pred[1024,16]{0,1:T(8,128)(4,1)}, pred[1024,16]{0,1:T(8,128)(4,1)S(1)}, u32[]{:S(2)}) copy-start(pred[1024,16]{0,1:T(8,128)(4,1)S(1)} %broadcast_compare_fusion.1) | copy-start | bytes 49156
  189.7 5.7 %copy-start.12 = (pred[448]{0:T(512)(128)(4,1)}, pred[448]{0:T(512)(128)(4,1)S(1)}, u32[]{:S(2)}) copy-start(pred[448]{0:T(512)(128)(4,1)S(1)} %iota_compare_fusion) | copy-start | bytes 1348
  192.2 3.3 copy-start.8
  196.4 16.6 %all-to-all-start.2 = ((f32[2,64,16]{2,0,1:T(2,128)}), f32[2,64,16]{2,0,1:T(2,128)S(1)}, u32[]{:S(2)}, u32[]{:S(2)}) async-start(f32[2,64,16]{2,0,1:T(2,128)} %copy.100), calls=%async_computation.2 | async-start | bytes 131072 | tf_op jit(solution)/shard_map/all_to_all | solution.py:152
  213.1 0.6 copy-start.6
  213.7 16.7 %all-to-all-start.1 = ((f32[2,64,16]{2,0,1:T(2,128)}), f32[2,64,16]{2,0,1:T(2,128)S(1)}, u32[]{:S(2)}, u32[]{:S(2)}) async-start(f32[2,64,16]{2,0,1:T(2,128)} %copy.99), calls=%async_computation.1 | async-start | bytes 131072 | tf_op jit(solution)/shard_map/all_to_all | solution.py:145
  219.3 19.4 %copy-start.7 = (f32[2,64,16]{2,0,1:T(2,128)S(1)}, f32[2,64,16]{2,0,1:T(2,128)}, u32[]{:S(2)}) copy-start(f32[2,64,16]{2,0,1:T(2,128)} %copy-done.6) | copy-start | bytes 24580
  230.4 35.9 %all-to-all-start = ((f32[2,64,16,128]{3,2,0,1:T(8,128)}), f32[2,64,16,128]{3,2,0,1:T(8,128)S(1)}, u32[]{:S(2)}, u32[]{:S(2)}) async-start(f32[2,64,16,128]{3,2,0,1:T(8,128)} %copy.98), calls=%async_computation | async-start | bytes 2097152 | tf_op jit(solution)/shard_map/all_to_all | solution.py:159
  234.9 101.8 %reduce-scatter.2.cloned.1.call-start = ((), (), s32[]{:S(2)}) async-start(), calls=%async_computation.7 | async-start | bytes 663552 | tf_op jit(solution)/shard_map/reduce_scatter | solution.py:180
  271.9 3.2 copy-start.1
  290.7 4.6 %copy-start.2 = (f32[2,128,8192]{2,1,0:T(8,128)S(1)}, f32[2,128,8192]{2,1,0:T(8,128)}, u32[]{:S(2)}) copy-start(f32[2,128,8192]{2,1,0:T(8,128)} %copy-done.1) | copy-start | bytes 25165828
  295.4 11.5 %copy-start.3 = (bf16[128,2,128]{2,0,1:T(8,128)(2,1)S(1)}, bf16[128,2,128]{2,0,1:T(8,128)(2,1)}, u32[]{:S(2)}) copy-start(bf16[128,2,128]{2,0,1:T(8,128)(2,1)} %fusion.43) | copy-start | bytes 196612
  297.7 54.5 %copy-start.5 = (bf16[2,1,64,256]{3,2,1,0:T(8,128)(2,1)S(1)}, bf16[2,1,64,256]{3,2,1,0:T(8,128)(2,1)}, u32[]{:S(2)}) copy-start(bf16[2,1,64,256]{3,2,1,0:T(8,128)(2,1)} %param.11) | copy-start | bytes 196612
  297.7 54.5 %copy-start.10 = (bf16[2,1,8,256]{3,2,1,0:T(8,128)(2,1)S(1)}, bf16[2,1,8,256]{3,2,1,0:T(8,128)(2,1)}, u32[]{:S(2)}) copy-start(bf16[2,1,8,256]{3,2,1,0:T(8,128)(2,1)} %param.12) | copy-start | bytes 24580
  297.7 54.5 %copy-start.15 = (f32[256]{0:T(256)S(1)}, f32[256]{0:T(256)}, u32[]{:S(2)}) copy-start(f32[256]{0:T(256)} %param.21) | copy-start | bytes 3076
  299.6 19.4 %all-to-all-start.4 = ((bf16[2,64,1,256]{3,0,2,1:T(2,128)(2,1)}), bf16[2,64,1,256]{3,0,2,1:T(2,128)(2,1)S(1)}, u32[]{:S(2)}, u32[]{:S(2)}) async-start(bf16[2,64,1,256]{3,0,2,1:T(2,128)(2,1)} %copy.106), calls=%async_computation.5 | async-start | bytes 131072 | tf_op jit(solution)/shard_map/all_to_all | solution.py:207
  319.0 16.8 %all-to-all-start.3 = ((bf16[2,64,1,256]{3,0,2,1:T(2,128)(2,1)}), bf16[2,64,1,256]{3,0,2,1:T(2,128)(2,1)S(1)}, u32[]{:S(2)}, u32[]{:S(2)}) async-start(bf16[2,64,1,256]{3,0,2,1:T(2,128)(2,1)} %copy.103), calls=%async_computation.4 | async-start | bytes 131072 | tf_op jit(solution)/shard_map/all_to_all | solution.py:206
Sparse Core Ops, SparseCore 0:
  77.5 106.5 all-gather.6
  187.5 103.2 all-gather.4
  299.0 33.8 reduce-scatter.1
where the time goes:
time: 364 us; the launch traced here: 361 us
  blocking collectives  184 us (51%)
  waiting for transfers between devices  82 us (23%)
  starting transfers between devices  25.2 us (7%)
  matrix products  20.2 us (6%)
  local copies, waits for them, and re-layouts  18.7 us (5%)
  other arithmetic  16.3 us (4%)
  between operations  14.3 us (4%)
    all_gather x1, blocking collectives, per_device(): all_queries = lax.all_gather(query_cont[None], 'seq', axis=0, tiled=True)  106 us
    all_to_all x1, waiting for transfers between devices, per_device(): lax.all_to_all(cont_out.reshape(head_count, seq_count, cont_rows, HD), 's...  26.2 us
    all_gather x1, blocking collectives, per_device(): lax.all_gather(prompt_states, 'tp', axis=3, tiled=True)  24.9 us
    all_gather x1, blocking collectives, per_device(): lax.all_gather(cont_states, 'tp', axis=3, tiled=True)  23.7 us
    all_gather x1, waiting for transfers between devices, per_device(): lax.all_gather(value_prompt[None], 'seq', axis=0, tiled=True)  15.5 us
    psum x1, blocking collectives, per_device(): lax.psum((jnp.sum(query_proj * query_proj, -1), jnp.sum(key_proj * key_pr...  15.1 us
    psum x1, blocking collectives, per_device(): proj_sq = lax.psum(jnp.sum(projected * projected, -1), 'tp')  14.4 us
    all_to_all x1, waiting for transfers between devices, per_device(): lax.all_to_all(to_cyclic(key_prompt), 'seq', split_axis=1, concat_axis=1,...  12.1 us
  transfers between devices with their start and end apart: 8, of which 6 were waited for; matrix products, arithmetic and copies ran while one was open for 10% of the time, Pallas kernels for 0%

commit v1 on v0

v1 whole, which is shorter than its diff:
```python
import math
import jax
import jax.numpy as jnp
import numpy as np
from jax import lax
from jax.experimental import pallas as pl
from jax.experimental.pallas import tpu as pltpu
from jax.sharding import PartitionSpec as P

HD = 128
EPS = 1e-06
THETA = 500000.0
NEG = -1e30
ZN, YN, CN, TP = 4, 8, 2, 8
CHIPS = ZN * YN
BLK, CBLK, CAP = 64, 8, 448
ROWS = 2 * BLK
CROWS = 2 * CBLK
ALL = ROWS + CROWS
W = 256
D = 2048
CACHED = 14336
KEYS = YN * CN * BLK
CKEYS = 1024
MSG = W + 128
QSCALE = math.log2(math.e) / math.sqrt(HD)
F32, BF16 = jnp.float32, jnp.bfloat16


def iota(shape, dim):
    return lax.broadcasted_iota(jnp.int32, shape, dim)


def attend(q, k, v, allowed):
    s = lax.dot_general(q, k, (((1,), (1,)), ((), ())), preferred_element_type=F32)
    s = jnp.where(allowed, s, NEG)
    m = jnp.max(s, -1, keepdims=True).astype(BF16).astype(F32)
    p = jnp.exp2(s - jnp.maximum(m, -1e29))
    total = jnp.sum(p, -1, keepdims=True)
    out = jnp.dot(p.astype(BF16), v, preferred_element_type=F32)
    return out, m, total


def message(parts):
    rows = parts[0][0].shape[0]
    lane = iota((rows, 128), 1)
    stats = jnp.zeros((rows, 128), F32)
    for h, (_, m, total) in enumerate(parts):
        high = total.astype(BF16).astype(F32)
        stats = jnp.where(lane == 3 * h, m, stats)
        stats = jnp.where(lane == 3 * h + 1, high, stats)
        stats = jnp.where(lane == 3 * h + 2, total - high, stats)
    return jnp.concatenate([p[0].astype(BF16) for p in parts] + [stats.astype(BF16)], -1)


def combine(pieces):
    outs = []
    stats = [p[:, W:].astype(F32) for p in pieces]
    for h in range(2):
        ms = [s[:, 3 * h : 3 * h + 1] for s in stats]
        ls = [s[:, 3 * h + 1 : 3 * h + 2] + s[:, 3 * h + 2 : 3 * h + 3] for s in stats]
        top = ms[0]
        for m in ms[1:]:
            top = jnp.maximum(top, m)
        num, den = 0.0, 0.0
        for p, m, l in zip(pieces, ms, ls):
            w = jnp.exp2(m - top)
            num = num + w * p[:, h * HD : (h + 1) * HD].astype(F32)
            den = den + w * l
        outs.append(num / den)
    return jnp.concatenate(outs, -1).astype(BF16)


def kernel(
    prompt, cont, cache, lengths, wq_h, wk_h, wv_h, wo_h, qgain, kgain, pgain, inv,
    hid_p, hid_c, kv_out,
    wq, wk, wv, wo, xg, xc, cos, sin, sq_out, sq_in, qg, kvg, qcg, kcc,
    oc_out, oc_in, op_out, op_in, kv_s, kv_r, att, pr_out, pr_in,
    local, tp_ss, tp_rs, tpc_ss, tpc_rs, sq_ss, sq_rs, core_ss, core_rs,
    qc_ss, qc_rs, q_ss, q_rs, ring_ss, ring_rs, pair_ss, pair_rs,
    oc_ss, oc_rs, op_ss, op_rs, kv_ss, kv_rs, pr_ss, pr_rs,
):
    s_idx = lax.axis_index("seq")
    t = lax.axis_index("tp")
    z = s_idx // (YN * CN)
    y = (s_idx // CN) % YN
    c = s_idx % CN
    chip = s_idx // CN
    x, zl = t // 2, t % 2

    def seq_of(z_, y_, c_):
        return (z_ * YN + y_) * CN + c_

    def remote(src, dst, ss, rs, seq=None, tp=None):
        dev = {"seq": s_idx if seq is None else seq, "tp": t if tp is None else tp}
        return pltpu.make_async_remote_copy(
            src_ref=src, dst_ref=dst, send_sem=ss, recv_sem=rs,
            device_id=dev, device_id_type=pl.DeviceIdType.MESH,
        )

    partner = s_idx + 1 - 2 * c
    hops = [(0, 1), (1, 0), (3, 0), (1, 1), (3, 1), (2, 0), (2, 1)]
    peers = [((x + dx) % 4) * 2 + (zl + dz) % 2 for dx, dz in hops]

    loads = [
        pltpu.make_async_copy(prompt, xg.at[t], local.at[0]),
        pltpu.make_async_copy(cont, xc.at[t], local.at[1]),
        pltpu.make_async_copy(wq_h, wq, local.at[2]),
        pltpu.make_async_copy(wk_h, wk, local.at[3]),
        pltpu.make_async_copy(wv_h, wv, local.at[4]),
        pltpu.make_async_copy(
            cache, kcc.at[:, pl.ds(pl.multiple_of(c * CAP, 64), CAP), :], local.at[5]
        ),
    ] + [
        pltpu.make_async_copy(wo_h.at[:, i * W : (i + 1) * W], wo.at[i], local.at[6 + i])
        for i in range(TP)
    ]
    for load in loads:
        load.start()

    barrier = pltpu.get_barrier_semaphore()
    for p in peers:
        pl.semaphore_signal(
            barrier, inc=1, device_id={"seq": s_idx, "tp": p}, device_id_type=pl.DeviceIdType.MESH
        )
    pl.semaphore_signal(
        barrier, inc=1, device_id={"seq": partner, "tp": t}, device_id_type=pl.DeviceIdType.MESH
    )

    def greet(i, carry):
        other = ((chip + i) % CHIPS) * CN + c
        pl.semaphore_signal(
            barrier, inc=1, device_id={"seq": other, "tp": t}, device_id_type=pl.DeviceIdType.MESH
        )
        return carry

    lax.fori_loop(1, CHIPS, greet, 0)

    r = iota((ALL, 128), 0)
    low_p = s_idx * BLK + r
    high_p = (2 * CHIPS * CN - 1 - s_idx) * BLK + r - BLK
    low_c = CACHED + s_idx * CBLK + r - ROWS
    high_c = CACHED + (2 * CHIPS * CN - 1 - s_idx) * CBLK + r - ROWS - CBLK
    pos = jnp.where(
        r < BLK, low_p, jnp.where(r < ROWS, high_p, jnp.where(r < ROWS + CBLK, low_c, high_c))
    )
    angle = pos.astype(F32) * inv[...]
    cos[...] = jnp.cos(angle)
    sine = jnp.sin(angle)
    sin[...] = jnp.where(iota((ALL, 128), 1) < HD // 2, -sine, sine)
    pad0 = 2 * CAP + 2 * CROWS
    kcc[:, pad0:, :] = jnp.zeros((2, CKEYS - pad0, W), BF16)

    pl.semaphore_wait(barrier, len(peers) + 1 + CHIPS - 1)

    sends = []
    for i in (6, 5, 4, 3, 2, 1, 0):
        a = remote(prompt, xg.at[t], tp_ss.at[i], tp_rs.at[t], tp=peers[i])
        b = remote(cont, xc.at[t], tpc_ss.at[i], tpc_rs.at[t], tp=peers[i])
        a.start()
        b.start()
        sends += [a, b]
    cache_send = remote(
        cache, kcc.at[:, pl.ds(pl.multiple_of(c * CAP, 64), CAP), :],
        core_ss.at[0], core_rs.at[0], seq=partner,
    )
    cache_send.start()

    for load in loads[:5]:
        load.wait()
    qp = jnp.zeros((ALL, W), F32)
    kp = jnp.zeros((ALL, W), F32)
    vp = jnp.zeros((ALL, W), F32)
    for i in range(-1, 7):
        if i >= 0:
            src = peers[i]
            remote(prompt, xg.at[src], tp_ss.at[i], tp_rs.at[src], tp=src).wait_recv()
            remote(cont, xc.at[src], tpc_ss.at[i], tpc_rs.at[src], tp=src).wait_recv()
        else:
            src = t
        rows = jnp.concatenate(
            [
                xg[src].reshape(ROWS, W),
                xc[src].astype(F32).reshape(CROWS, W).astype(BF16),
            ],
            0,
        )
        ks = pl.ds(pl.multiple_of(src * W, W), W)
        qp += jnp.dot(rows, wq[ks, :], preferred_element_type=F32)
        kp += jnp.dot(rows, wk[ks, :], preferred_element_type=F32)
        vp += jnp.dot(rows, wv[ks, :], preferred_element_type=F32)

    lane = iota((ALL, 128), 1)

    def total_squares(columns, phase):
        stat = jnp.zeros((ALL, 128), F32)
        for j, col in enumerate(columns):
            stat = jnp.where(lane == j, col, stat)
        stat = jnp.concatenate([stat, jnp.zeros((256 - ALL, 128), F32)], 0)
        mine = stat.T[:8, :]
        sq_out[phase] = mine
        out = []
        for i in range(7):
            d = remote(
                sq_out.at[phase], sq_in.at[phase, t], sq_ss.at[phase, i], sq_rs.at[phase, t],
                tp=peers[i],
            )
            d.start()
            out.append(d)
        total = mine
        for i in range(7):
            remote(
                sq_out.at[phase], sq_in.at[phase, peers[i]], sq_ss.at[phase, i],
                sq_rs.at[phase, peers[i]], tp=peers[i],
            ).wait_recv()
            total = total + sq_in[phase, peers[i]]
        back = jnp.concatenate([total, jnp.zeros((120, 256), F32)], 0).T
        return [back[:ALL, j : j + 1] for j in range(len(columns))], out

    (q_sq, k_sq), more = total_squares(
        [jnp.sum(qp * qp, -1, keepdims=True), jnp.sum(kp * kp, -1, keepdims=True)], 0
    )
    sends += more
    qn = qp * lax.rsqrt(q_sq / D + EPS) * qgain[...]
    kn = kp * lax.rsqrt(k_sq / D + EPS) * kgain[...]

    def rotate(field, scale):
        outs = []
        for h in range(2):
            f = field[:, h * HD : (h + 1) * HD]
            g = f * cos[...] + pltpu.roll(f, HD // 2, 1) * sin[...]
            outs.append((g * scale if scale is not None else g).astype(BF16))
        return jnp.concatenate(outs, -1)

    queries = rotate(qn, QSCALE)
    keys = rotate(kn, None)
    values = vp.astype(BF16)
    here = YN * 0 + 2 * y + c
    own = pl.ds(pl.multiple_of(here * BLK, BLK), BLK)
    qcg[chip] = queries[ROWS:]
    qg[z] = queries[:ROWS]
    for kv, field in ((0, keys), (1, values)):
        kvg[kv, 0, own, :] = field[:BLK]
        kvg[kv, 1, own, :] = field[BLK:ROWS]
        kcc[kv, pl.ds(pl.multiple_of(2 * CAP + c * CROWS, CROWS), CROWS), :] = field[ROWS:]

    def cont_q(i, other):
        return remote(qcg.at[chip], qcg.at[chip], qc_ss.at[i], qc_rs.at[chip],
                      seq=other * CN + c)

    def start_cont_q(i, carry):
        cont_q(i, (chip + i) % CHIPS).start()
        return carry

    lax.fori_loop(1, CHIPS, start_cont_q, 0)
    new_rows = kcc.at[:, pl.ds(pl.multiple_of(2 * CAP + c * CROWS, CROWS), CROWS), :]
    new_send = remote(new_rows, new_rows, core_ss.at[1], core_rs.at[1], seq=partner)
    new_send.start()
    sends += [cache_send, new_send]

    for i in (2, 1, 3):
        d = remote(qg.at[z], qg.at[z], q_ss.at[i], q_rs.at[z], seq=seq_of((z + i) % ZN, y, c))
        d.start()
        sends.append(d)

    def piece(origin_y, core, kv):
        rows = pl.ds(pl.multiple_of((2 * origin_y + core) * BLK, BLK), BLK)
        return kvg.at[kv, :, rows, :]

    right, left = seq_of(z, (y + 1) % YN, c), seq_of(z, (y + YN - 1) % YN, c)

    def ring(direction, step, kv, origin):
        return remote(
            piece(origin, c, kv), piece(origin, c, kv), ring_ss.at[direction, step, kv],
            ring_rs.at[direction, step, kv], seq=right if direction == 0 else left,
        )

    def pair(origin, core, kv):
        return remote(
            piece(origin, core, kv), piece(origin, core, kv),
            pair_ss.at[origin, kv], pair_rs.at[origin, kv], seq=partner,
        )

    def launch(step):
        for kv in range(2):
            for direction in range(2):
                if step == 4 and kv != direction:
                    continue
                origin = (y + (YN - step + 1 if direction == 0 else step - 1)) % YN
                if step > 1:
                    ring(direction, step - 1, kv, origin).wait_recv()
                d = ring(direction, step, kv, origin)
                d.start()
                sends.append(d)
                if step > 1 or direction == 0:
                    e = pair(origin, c, kv)
                    e.start()
                    sends.append(e)
            if step == 4:
                other = 1 - kv
                origin = (y + (YN - 3 if other == 0 else 3)) % YN
                ring(other, 3, kv, origin).wait_recv()
                e = pair(origin, c, kv)
                e.start()
                sends.append(e)

    launch(1)
    launch(2)
    launch(3)

    loads[5].wait()
    remote(
        cache, kcc.at[:, pl.ds(pl.multiple_of((1 - c) * CAP, 64), CAP), :],
        core_ss.at[0], core_rs.at[0], seq=partner,
    ).wait_recv()
    other_rows = kcc.at[:, pl.ds(pl.multiple_of(2 * CAP + (1 - c) * CROWS, CROWS), CROWS), :]
    remote(other_rows, other_rows, core_ss.at[1], core_rs.at[1], seq=partner).wait_recv()

    def wait_cont_q(i, carry):
        other = (chip + i) % CHIPS
        remote(qcg.at[other], qcg.at[other], qc_ss.at[i], qc_rs.at[other],
               seq=other * CN + c).wait_recv()
        return carry

    lax.fori_loop(1, CHIPS, wait_cont_q, 0)
    n = iota((1, CKEYS), 1)
    dead = 1 << 30
    j = n - 2 * CAP
    key_dev = chip * CN + j // CROWS
    in_block = j % CROWS
    new_pos = jnp.where(
        in_block < CBLK,
        key_dev * CBLK + in_block,
        (2 * CHIPS * CN - 1 - key_dev) * CBLK + in_block - CBLK,
    )
    key_pos = jnp.where(
        n < CAP,
        jnp.where(n < lengths[chip * CN], -1, dead),
        jnp.where(
            n < 2 * CAP,
            jnp.where(n - CAP < lengths[chip * CN + 1], -1, dead),
            jnp.where(n < pad0, new_pos, dead),
        ),
    )

    def cont_block(b, carry):
        rq = b * 128 + iota((128, 1), 0)
        dev = (rq // CROWS) * CN + c
        off = rq % CROWS
        q_pos = jnp.where(
            off < CBLK, dev * CBLK + off, (2 * CHIPS * CN - 1 - dev) * CBLK + off - CBLK
        )
        allowed = key_pos <= q_pos
        q = qcg[pl.ds(b * 8, 8)].reshape(128, W)
        parts = [
            attend(
                q[:, h * HD : (h + 1) * HD],
                kcc[0, :, h * HD : (h + 1) * HD],
                kcc[1, :, h * HD : (h + 1) * HD],
                allowed,
            )
            for h in range(2)
        ]
        oc_out[pl.ds(b * 8, 8)] = message(parts).reshape(8, CROWS, MSG)
        return carry

    lax.fori_loop(0, 4, cont_block, 0)

    launch(4)

    def cont_o(i, other):
        return remote(oc_out.at[other], oc_in.at[chip], oc_ss.at[i], oc_rs.at[chip],
                      seq=other * CN + c)

    def start_cont_o(i, carry):
        cont_o(i, (chip + i) % CHIPS).start()
        return carry

    lax.fori_loop(1, CHIPS, start_cont_o, 0)

    far = (y + 4) % YN
    for kv in range(2):
        ring(kv, 4, kv, far).wait_recv()
        e = pair(far, c, kv)
        e.start()
        sends.append(e)
    for i in (2, 1, 3):
        src = (z + i) % ZN
        remote(qg.at[src], qg.at[src], q_ss.at[i], q_rs.at[src],
               seq=seq_of(src, y, c)).wait_recv()
    for origin in range(YN):
        for kv in range(2):
            remote(
                piece(origin, 1 - c, kv), piece(origin, 1 - c, kv),
                pair_ss.at[origin, kv], pair_rs.at[origin, kv], seq=partner,
            ).wait_recv()

    n2 = iota((1, 2 * KEYS), 1)
    hi_n = n2 - KEYS
    top = 2 * CHIPS * CN - 1
    key_pos2 = jnp.where(
        n2 < KEYS,
        z * KEYS + n2,
        (top - z * (YN * CN) - hi_n // BLK) * BLK + hi_n % BLK,
    )

    def prompt_block(i, carry):
        zq = (z + i) % ZN
        dev = zq * (YN * CN) + here
        rq = iota((ROWS, 1), 0)
        q_pos = jnp.where(rq < BLK, dev * BLK + rq, (top - dev) * BLK + rq - BLK)
        allowed = key_pos2 <= q_pos
        q = qg[zq]
        parts = [
            attend(
                q[:, h * HD : (h + 1) * HD],
                kvg[0, :, :, h * HD : (h + 1) * HD].reshape(2 * KEYS, HD),
                kvg[1, :, :, h * HD : (h + 1) * HD].reshape(2 * KEYS, HD),
                allowed,
            )
            for h in range(2)
        ]
        op_out[zq] = message(parts)
        return carry

    def prompt_o(i):
        return remote(op_out.at[(z + i) % ZN], op_in.at[z], op_ss.at[i], op_rs.at[z],
                      seq=seq_of((z + i) % ZN, y, c))

    for i in (2, 1, 3):
        prompt_block(i, 0)
        d = prompt_o(i)
        d.start()
        sends.append(d)
    prompt_block(0, 0)

    ro = iota((128, 2 * KEYS), 0)
    co = iota((128, 2 * KEYS), 1)
    jj = ro % 16
    want = (ro // 32) * 16 + here
    pick_row = jnp.where(ro % 32 < 16, jj * BLK, KEYS + (15 - jj) * BLK) + want
    onehot = jnp.where(co == pick_row, 1.0, 0.0).astype(BF16)
    for kv in range(2):
        rows = jnp.dot(onehot, kvg[kv].reshape(2 * KEYS, W), preferred_element_type=F32)
        kv_s[:, kv] = rows.astype(BF16).reshape(ZN, 2, 16, W)
    for i in (2, 1, 3):
        dst = (z + i) % ZN
        d = remote(kv_s.at[dst], kv_r.at[z], kv_ss.at[i], kv_rs.at[z], seq=seq_of(dst, y, c))
        d.start()
        sends.append(d)

    def wait_cont_o(i, carry):
        other = (chip + i) % CHIPS
        remote(oc_out.at[other], oc_in.at[other], oc_ss.at[i], oc_rs.at[other],
               seq=other * CN + c).wait_recv()
        return carry

    lax.fori_loop(1, CHIPS, wait_cont_o, 0)
    oc_in[chip] = oc_out[chip]
    att[ROWS:, :] = combine([oc_in[i] for i in range(CHIPS)])
    for i in (1, 3, 2):
        src = (z + i) % ZN
        remote(op_out.at[src], op_in.at[src], op_ss.at[i], op_rs.at[src],
               seq=seq_of(src, y, c)).wait_recv()
    att[:ROWS, :] = combine([op_out[z]] + [op_in[(z + i) % ZN] for i in (1, 3, 2)])

    for load in loads[6:]:
        load.wait()
    a = att[...]
    for i in (6, 5, 4, 3, 2, 1, 0):
        p = peers[i]
        pr_out[p] = jnp.dot(a, wo[p], preferred_element_type=F32).astype(BF16)
        d = remote(pr_out.at[p], pr_in.at[t], pr_ss.at[i], pr_rs.at[t], tp=p)
        d.start()
        sends.append(d)
    proj = jnp.dot(a, wo[t], preferred_element_type=F32).astype(BF16).astype(F32)
    for i in range(7):
        p = peers[i]
        remote(pr_out.at[p], pr_in.at[p], pr_ss.at[i], pr_rs.at[p], tp=p).wait_recv()
        proj = proj + pr_in[p].astype(F32)

    (p_sq,), more = total_squares([jnp.sum(proj * proj, -1, keepdims=True)], 1)
    sends += more
    normed = proj * lax.rsqrt(p_sq / D + EPS) * pgain[...]
    hid_p[...] = (xg[t].astype(F32) + normed[:ROWS].reshape(2, BLK, W)).astype(BF16)
    hid_c[...] = (xc[t].astype(F32) + normed[ROWS:].reshape(2, CBLK, W)).astype(BF16)

    for i in (1, 3, 2):
        src = (z + i) % ZN
        remote(kv_s.at[src], kv_r.at[src], kv_ss.at[i], kv_rs.at[src],
               seq=seq_of(src, y, c)).wait_recv()
    kv_r[z] = kv_s[z]
    for src in range(ZN):
        for kv in range(2):
            kv_out[kv, 16 * src : 16 * src + 16, :] = kv_r[src, kv, 0]
            kv_out[kv, 112 - 16 * src : 128 - 16 * src, :] = kv_r[src, kv, 1]

    for d in sends:
        d.wait_send()

    def drain(i, carry):
        cont_q(i, (chip + i) % CHIPS).wait_send()
        cont_o(i, (chip + i) % CHIPS).wait_send()
        return carry

    lax.fori_loop(1, CHIPS, drain, 0)


def per_device(
    prompt_states, cont_states, cache_kv, cache_lengths, w_query, w_key, w_value, w_out,
    q_gain, k_gain, post_gain,
):
    half = HD // 2
    freq = THETA ** (-(np.arange(half) * 2.0 / HD))
    inv = jnp.asarray(np.concatenate([freq, freq])[None, :].astype(np.float32))
    any_ = pl.BlockSpec(memory_space=pl.ANY)
    vmem = pl.BlockSpec(memory_space=pltpu.VMEM)
    smem = pl.BlockSpec(memory_space=pltpu.SMEM)
    dma = pltpu.SemaphoreType.DMA
    hid_p, hid_c, kv = pl.pallas_call(
        kernel,
        out_shape=(
            jax.ShapeDtypeStruct((2, BLK, W), BF16),
            jax.ShapeDtypeStruct((2, CBLK, W), BF16),
            jax.ShapeDtypeStruct((2, 2 * BLK, W), BF16),
        ),
        in_specs=[any_, any_, any_, smem, any_, any_, any_, any_, vmem, vmem, vmem, vmem],
        out_specs=(vmem, vmem, vmem),
        scratch_shapes=[
            pltpu.VMEM((D, W), BF16),
            pltpu.VMEM((D, W), BF16),
            pltpu.VMEM((D, W), BF16),
            pltpu.VMEM((TP, W, W), BF16),
            pltpu.VMEM((TP, 2, BLK, W), BF16),
            pltpu.VMEM((TP, 2, CBLK, W), BF16),
            pltpu.VMEM((ALL, 128), F32),
            pltpu.VMEM((ALL, 128), F32),
            pltpu.VMEM((2, 8, 256), F32),
            pltpu.VMEM((2, TP, 8, 256), F32),
            pltpu.VMEM((ZN, ROWS, W), BF16),
            pltpu.VMEM((2, 2, KEYS, W), BF16),
            pltpu.VMEM((CHIPS, CROWS, W), BF16),
            pltpu.VMEM((2, CKEYS, W), BF16),
            pltpu.VMEM((CHIPS, CROWS, MSG), BF16),
            pltpu.VMEM((CHIPS, CROWS, MSG), BF16),
            pltpu.VMEM((ZN, ROWS, MSG), BF16),
            pltpu.VMEM((ZN, ROWS, MSG), BF16),
            pltpu.VMEM((ZN, 2, 2, 16, W), BF16),
            pltpu.VMEM((ZN, 2, 2, 16, W), BF16),
            pltpu.VMEM((ALL, W), BF16),
            pltpu.VMEM((TP, ALL, W), BF16),
            pltpu.VMEM((TP, ALL, W), BF16),
            dma((6 + TP,)),
            dma((7,)), dma((TP,)), dma((7,)), dma((TP,)),
            dma((2, 7)), dma((2, TP)),
            dma((2,)), dma((2,)),
            dma((CHIPS,)), dma((CHIPS,)),
            dma((ZN,)), dma((ZN,)),
            dma((2, 5, 2)), dma((2, 5, 2)),
            dma((YN, 2)), dma((YN, 2)),
            dma((CHIPS,)), dma((CHIPS,)),
            dma((ZN,)), dma((ZN,)),
            dma((ZN,)), dma((ZN,)),
            dma((7,)), dma((TP,)),
        ],
        compiler_params=pltpu.CompilerParams(
            collective_id=0, has_side_effects=True, vmem_limit_bytes=60 * 1024 * 1024
        ),
        name="block",
    )(
        prompt_states[:, 0], cont_states[:, 0], cache_kv[:, 0], cache_lengths,
        w_query, w_key, w_value, w_out,
        q_gain[None], k_gain[None], post_gain[None], inv,
    )
    return hid_p[:, None], hid_c[:, None], kv[:, None]


def solution(mesh):
    return jax.shard_map(
        per_device,
        mesh=mesh,
        in_specs=(
            P(None, "seq", None, "tp"),
            P(None, "seq", None, "tp"),
            P(None, "seq", None, "tp"),
            P(),
            P(None, "tp"),
            P(None, "tp"),
            P(None, "tp"),
            P("tp", None),
            P("tp"),
            P("tp"),
            P("tp"),
        ),
        out_specs=(
            P(None, "seq", None, "tp"),
            P(None, "seq", None, "tp"),
            P(None, "seq", None, "tp"),
        ),
        check_vma=False,
    )
```

time: 364 us -> 92.3 us (0.25)
  blocking collectives: 184 us -> 0 us
  Pallas kernels: 0 us -> 88.7 us
  waiting for transfers between devices: 82 us -> 0 us
  starting transfers between devices: 25.2 us -> 0 us
  matrix products: 20.2 us -> 0 us
  other arithmetic: 16.3 us -> 0 us
  local copies, waits for them, and re-layouts: 18.7 us -> 2.78 us
  between operations: 14.3 us -> 0.66 us
    all_gather x3 -> x0, blocking collectives: 155 us -> none  [the longest x1 106 us: per_device(): all_queries = lax.all_gather(query_cont[None], 'seq', axis=0, tiled=True)]
    pallas_call x0 -> x1, Pallas kernels: none -> 88.7 us  [per_device(): pl.pallas_call(kernel, out_shape=(jax.ShapeDtypeStruct((2, BLK, W), BF16)...]
    all_to_all x5 -> x0, waiting for transfers between devices: 66.4 us -> none  [the longest x1 26.2 us: per_device(): lax.all_to_all(cont_out.reshape(head_count, seq_count, cont_rows, HD), 's...]
    psum x2 -> x0, blocking collectives: 29.5 us -> none  [the longest x1 15.1 us: per_device(): lax.psum((jnp.sum(query_proj * query_proj, -1), jnp.sum(key_proj * key_pr...]
    all_to_all x5 -> x0, starting transfers between devices: 24.9 us -> none  [the longest x1 7.24 us: per_device(): lax.all_to_all(to_cyclic(value_prompt), 'seq', split_axis=1, concat_axis=...]
    dot_general x10 -> x0, matrix products: 20.2 us -> none  [the longest x3 7.36 us: absorb(): jnp.einsum('rhd,khd->hrk', queries, keys, preferred_element_type=jnp.floa...]
    all_gather x2 -> x0, waiting for transfers between devices: 15.6 us -> none  [the longest x1 15.5 us: per_device(): lax.all_gather(value_prompt[None], 'seq', axis=0, tiled=True)]
    reduce_sum x6 -> x0, other arithmetic: 7.95 us -> none  [the longest x3 5.3 us: absorb(): running_sum = running_sum * shrink + jnp.sum(weights, -1)]
  transfers between devices with their start and end apart: 8 -> 0, of which waited for: 6 -> 0; matrix products, arithmetic and copies ran while one was open for 10% -> 0% of each run, Pallas kernels for 0% -> 0%
where the time goes in v1:
time: 92.3 us; the launch traced here: 92.1 us
  Pallas kernels  88.7 us (96%)
  local copies, waits for them, and re-layouts  2.78 us (3%)
    pallas_call x1, Pallas kernels, per_device(): pl.pallas_call(kernel, out_shape=(jax.ShapeDtypeStruct((2, BLK, W), BF16)...  88.7 us
    unnamed x7, local copies, waits for them, and re-layouts  2.78 us

profile of v1, /device:TPU:1, one launch (start us, length us, event | category | flops | bytes accessed | tf_op | source)
XLA Modules:
  0.0 92.1 jit_solution(4376098705002872324)
XLA Ops:
  0.6 88.7 %block.1 = (bf16[2,64,256]{2,1,0:T(8,128)(2,1)}, bf16[2,8,256]{2,1,0:T(8,128)(2,1)}, bf16[2,128,256]{2,1,0:T(8,128)(2,1)}) custom-call(bf16[2,64,256]{2,1,0:T(8,128)(2,1)} %bitcast.17, bf16[2,8,256]{2,1,0:T(8,128)(2,1)} %bitcast.19, bf16[2,448,256]{2,1,0:T(8,128)(2,1)} %bitcast.15, s32[64]{0:T(128)} %lengths.1, bf16[2048,256]{1,0:T(8,128)(2,1)} %wq_h.1, ...), custom_call_target="tpu_custom_call" | custom-call | tf_op jit(solution)/shard_map/block/pallas_call | solution.py:520
  89.4 0.0 copy-start
  89.4 0.0 copy-start.1
  89.4 1.5 %copy.21 = bf16[2,1,64,256]{3,2,1,0:T(8,128)(2,1)} copy(bf16[2,1,64,256]{3,2,1,0:T(8,128)(2,1)} %bitcast.18) | data formatting | bytes 131072
  90.9 0.0 copy-done.1
  90.9 0.6 copy.22
  91.5 0.0 copy-done
  91.5 0.7 copy.23
Async XLA Ops:
  89.4 2.1 %copy-start = (bf16[2,128,256]{2,1,0:T(8,128)(2,1)S(1)}, bf16[2,128,256]{2,1,0:T(8,128)(2,1)}, u32[]{:S(2)}) copy-start(bf16[2,128,256]{2,1,0:T(8,128)(2,1)} %get-tuple-element.8) | copy-start | bytes 393220
  89.4 1.5 %copy-start.1 = (bf16[2,8,256]{2,1,0:T(8,128)(2,1)S(1)}, bf16[2,8,256]{2,1,0:T(8,128)(2,1)}, u32[]{:S(2)}) copy-start(bf16[2,8,256]{2,1,0:T(8,128)(2,1)} %get-tuple-element.7) | copy-start | bytes 24580

commit v2 on v1

v2 whole, which is shorter than its diff:
```python
import math
import jax
import jax.numpy as jnp
import numpy as np
from jax import lax
from jax.experimental import pallas as pl
from jax.experimental.pallas import tpu as pltpu
from jax.sharding import PartitionSpec as P

HD = 128
EPS = 1e-06
THETA = 500000.0
NEG = -1e30
ZN, YN, CN, TP = 4, 8, 2, 8
BLK, CBLK, CAP = 64, 8, 448
ROWS = 2 * BLK
CROWS = 2 * CBLK
ALL = ROWS + CROWS
W = 256
D = 2048
CACHED = 14336
KEYS = YN * CN * BLK
QUAD = 4
CGROUP = ZN * YN // 2
CKEYS = 1920
MSG = W + 128
QSCALE = math.log2(math.e) / math.sqrt(HD)
F32, BF16 = jnp.float32, jnp.bfloat16


def iota(shape, dim):
    return lax.broadcasted_iota(jnp.int32, shape, dim)


def attend(q, k, v, allowed, k_scale=None):
    s = lax.dot_general(q, k, (((1,), (1,)), ((), ())), preferred_element_type=F32)
    if k_scale is not None:
        s = s * k_scale
    s = jnp.where(allowed, s, NEG)
    m = jnp.max(s, -1, keepdims=True).astype(BF16).astype(F32)
    p = jnp.exp2(s - jnp.maximum(m, -1e29))
    total = jnp.sum(p, -1, keepdims=True)
    out = jnp.dot(p.astype(BF16), v, preferred_element_type=F32)
    return out, m, total


def message(parts):
    rows = parts[0][0].shape[0]
    lane = iota((rows, 128), 1)
    stats = jnp.zeros((rows, 128), F32)
    for h, (_, m, total) in enumerate(parts):
        high = total.astype(BF16).astype(F32)
        stats = jnp.where(lane == 3 * h, m, stats)
        stats = jnp.where(lane == 3 * h + 1, high, stats)
        stats = jnp.where(lane == 3 * h + 2, total - high, stats)
    return jnp.concatenate([p[0].astype(BF16) for p in parts] + [stats.astype(BF16)], -1)


def combine(pieces, stats):
    outs = []
    for h in range(2):
        top = stats[0][h][0]
        for st in stats[1:]:
            top = jnp.maximum(top, st[h][0])
        num, den = 0.0, 0.0
        for p, st in zip(pieces, stats):
            w = jnp.exp2(st[h][0] - top)
            num = num + w * p[:, h * HD : (h + 1) * HD].astype(F32)
            den = den + w * st[h][1]
        outs.append(num / den)
    return jnp.concatenate(outs, -1).astype(BF16)


def message_stats(piece):
    st = piece[:, W:].astype(F32)
    return [
        (st[:, 3 * h : 3 * h + 1], st[:, 3 * h + 1 : 3 * h + 2] + st[:, 3 * h + 2 : 3 * h + 3])
        for h in range(2)
    ]


def kernel(
    prompt, cont, cache, lengths, wq_h, wk_h, wv_h, wo_h, qgain, kgain, pgain, inv,
    hid_p, hid_c, kv_out,
    wq, wk, wv, wo, xg, xc, cos, sin, sq_out, sq_in, qg, kvg, qcg, kcc,
    oc_out, oc_in, op_out, op_in, os_out, os_in, kv_s, kv_r, att, pr_out, pr_in,
    ks_out, ks_in,
    local, tp_ss, tp_rs, tpc_ss, tpc_rs, sq_ss, sq_rs, cache_ss, cache_rs, new_ss, new_rs, ready,
    qc_ss, qc_rs, q_ss, q_rs, ring_ss, ring_rs, pair_ss, pair_rs,
    oc_ss, oc_rs, op_ss, op_rs, os_ss, os_rs, kv_ss, kv_rs, pr_ss, pr_rs,
    ks_ss, ks_rs,
):
    s_idx = lax.axis_index("seq")
    t = lax.axis_index("tp")
    z = s_idx // (YN * CN)
    y = (s_idx // CN) % YN
    c = s_idx % CN
    x, zl = t // 2, t % 2

    def seq_of(z_, y_, c_):
        return (z_ * YN + y_) * CN + c_

    def remote(src, dst, ss, rs, seq=None, tp=None):
        dev = {"seq": s_idx if seq is None else seq, "tp": t if tp is None else tp}
        return pltpu.make_async_remote_copy(
            src_ref=src, dst_ref=dst, send_sem=ss, recv_sem=rs,
            device_id=dev, device_id_type=pl.DeviceIdType.MESH,
        )

    partner = s_idx + 1 - 2 * c
    b = y % 2
    slot = 2 * b + c
    base = s_idx - slot
    twin = seq_of(z, y + 1 - 2 * b, c)
    cross = seq_of(z, y + 1 - 2 * b, 1 - c)
    twin_slot = 2 * (1 - b) + c
    group = z * (YN // 2) + y // 2

    def member(i):
        return seq_of(i // (YN // 2), (i % (YN // 2)) * 2 + b, c)

    def cache_rows(j):
        return kcc.at[:, pl.ds(pl.multiple_of(j * CAP, 64), CAP), :]

    def new_rows(j):
        return kcc.at[:, pl.ds(pl.multiple_of(QUAD * CAP + j * CROWS, CROWS), CROWS), :]

    hops = [(0, 1), (1, 0), (3, 0), (1, 1), (3, 1), (2, 0), (2, 1)]
    peers = [((x + dx) % 4) * 2 + (zl + dz) % 2 for dx, dz in hops]

    loads = [
        pltpu.make_async_copy(prompt, xg.at[t], local.at[0]),
        pltpu.make_async_copy(cont, xc.at[t], local.at[1]),
        pltpu.make_async_copy(wq_h, wq, local.at[2]),
        pltpu.make_async_copy(wk_h, wk, local.at[3]),
        pltpu.make_async_copy(wv_h, wv, local.at[4]),
        pltpu.make_async_copy(cache, cache_rows(slot), local.at[5]),
    ] + [
        pltpu.make_async_copy(wo_h.at[:, i * W : (i + 1) * W], wo.at[i], local.at[6 + i])
        for i in range(TP)
    ]
    for load in loads:
        load.start()

    def signal(sem, seq, tp):
        pl.semaphore_signal(
            sem, inc=1, device_id={"seq": seq, "tp": tp}, device_id_type=pl.DeviceIdType.MESH
        )

    barrier = pltpu.get_barrier_semaphore()
    here = 2 * y + c
    greeted = [(s_idx, p) for p in peers]
    greeted += [(z * (YN * CN) + (here + i) % (YN * CN), t) for i in range(1, YN * CN)]
    greeted += [(seq_of((z + i) % ZN, y, c), t) for i in (1, 2, 3)]
    for seq, tp in greeted:
        signal(barrier, seq, tp)

    pl.semaphore_wait(barrier, len(greeted))
    for i in (1, 2, 3):
        signal(ready, seq_of((z + i) % ZN, y, c), t)

    sends = []
    def go(*copies):
        for d in copies:
            d.start()
            sends.append(d)

    def rows_to(i):
        return remote(prompt, xg.at[t], tp_ss.at[i], tp_rs.at[t], tp=peers[i])

    def new_to(i):
        return remote(cont, xc.at[t], tpc_ss.at[i], tpc_rs.at[t], tp=peers[i])

    for i in (6, 5, 4, 3, 2, 1, 0):
        go(rows_to(i), new_to(i))
    for i, seq in ((0, twin), (1, partner)):
        d = remote(cache, cache_rows(slot), cache_ss.at[i], cache_rs.at[slot], seq=seq)
        d.start()
        sends.append(d)

    r = iota((ALL, 128), 0)
    low_p = s_idx * BLK + r
    high_p = (2 * CN * YN * ZN - 1 - s_idx) * BLK + r - BLK
    low_c = CACHED + s_idx * CBLK + r - ROWS
    high_c = CACHED + (2 * CN * YN * ZN - 1 - s_idx) * CBLK + r - ROWS - CBLK
    pos = jnp.where(
        r < BLK, low_p, jnp.where(r < ROWS, high_p, jnp.where(r < ROWS + CBLK, low_c, high_c))
    )
    angle = pos.astype(F32) * inv[...]
    cos[...] = jnp.cos(angle)
    sine = jnp.sin(angle)
    sin[...] = jnp.where(iota((ALL, 128), 1) < HD // 2, -sine, sine)
    pad0 = QUAD * (CAP + CROWS)
    kcc[:, pad0:, :] = jnp.zeros((2, CKEYS - pad0, W), BF16)

    for load in loads[:5]:
        load.wait()
    qp = jnp.zeros((ALL, W), F32)
    kp = jnp.zeros((ALL, W), F32)
    vp = jnp.zeros((ALL, W), F32)
    for i in range(-1, 7):
        if i < 0:
            src = t
        else:
            src = peers[i]
            remote(prompt, xg.at[src], tp_ss.at[i], tp_rs.at[src], tp=src).wait_recv()
            remote(cont, xc.at[src], tpc_ss.at[i], tpc_rs.at[src], tp=src).wait_recv()
        rows = jnp.concatenate(
            [
                xg[src].reshape(ROWS, W),
                xc[src].astype(F32).reshape(CROWS, W).astype(BF16),
            ],
            0,
        )
        ks = pl.ds(pl.multiple_of(src * W, W), W)
        qp += jnp.dot(rows, wq[ks, :], preferred_element_type=F32)
        kp += jnp.dot(rows, wk[ks, :], preferred_element_type=F32)
        vp += jnp.dot(rows, wv[ks, :], preferred_element_type=F32)

    lane = iota((ALL, 128), 1)

    def send_squares(columns, phase):
        stat = jnp.zeros((ALL, 128), F32)
        for j, col in enumerate(columns):
            stat = jnp.where(lane == j, col, stat)
        stat = jnp.concatenate([stat, jnp.zeros((256 - ALL, 128), F32)], 0)
        sq_out[phase] = stat.T[:8, :]
        for i in (6, 5, 4, 3, 2, 1, 0):
            d = remote(
                sq_out.at[phase], sq_in.at[phase, t], sq_ss.at[phase, i], sq_rs.at[phase, t],
                tp=peers[i],
            )
            d.start()
            sends.append(d)

    def total_squares(count, phase):
        total = sq_out[phase]
        for i in range(7):
            remote(
                sq_out.at[phase], sq_in.at[phase, peers[i]], sq_ss.at[phase, i],
                sq_rs.at[phase, peers[i]], tp=peers[i],
            ).wait_recv()
            total = total + sq_in[phase, peers[i]]
        back = jnp.concatenate([total, jnp.zeros((120, 256), F32)], 0).T
        return [back[:ALL, j : j + 1] for j in range(count)]

    send_squares([jnp.sum(qp * qp, -1, keepdims=True), jnp.sum(kp * kp, -1, keepdims=True)], 0)

    own = pl.ds(pl.multiple_of(here * BLK, BLK), BLK)

    def rotate(field):
        outs = []
        for h in range(2):
            f = field[:, h * HD : (h + 1) * HD]
            outs.append(f * cos[...] + pltpu.roll(f, HD // 2, 1) * sin[...])
        return jnp.concatenate(outs, -1)

    def keep(kv, field):
        kvg[kv, 0, own, :] = field[:BLK]
        kvg[kv, 1, own, :] = field[BLK:ROWS]

    def piece(origin_y, core, kv, half):
        rows = pl.ds(pl.multiple_of((2 * origin_y + core) * BLK, BLK), BLK)
        return kvg.at[kv, half, rows, :]

    def along(hop, direction, dist, kv, half, origin):
        step = dist if direction == 0 else YN - dist
        return remote(
            piece(origin, c, kv, half), piece(origin, c, kv, half),
            ring_ss.at[direction, hop, kv, half], ring_rs.at[direction, hop, kv, half],
            seq=seq_of(z, (y + step) % YN, c),
        )

    def pair(origin, core, kv, half):
        return remote(
            piece(origin, core, kv, half), piece(origin, core, kv, half),
            pair_ss.at[origin, kv, half], pair_rs.at[origin, kv, half], seq=partner,
        )

    def start_pair(origin, kv, half):
        d = pair(origin, c, kv, half)
        d.start()
        sends.append(d)

    def launch(kv):
        for dist in (2, 1):
            for half in range(2):
                for direction in range(2):
                    go(along(dist, direction, dist, kv, half, y))
        for half in range(2):
            start_pair(y, kv, half)

    def came_from(direction, dist):
        return (y + (YN - dist if direction == 0 else dist)) % YN

    def forward(kv):
        for half in range(2):
            for direction in range(2):
                origin = came_from(direction, 2)
                along(2, direction, 2, kv, half, origin).wait_recv()
                if direction == half:
                    go(along(4, direction, 2, kv, half, origin))
                go(along(3, direction, 1, kv, half, origin))
                start_pair(origin, kv, half)
        for half in range(2):
            for direction in range(2):
                origin = came_from(direction, 1)
                along(1, direction, 1, kv, half, origin).wait_recv()
                start_pair(origin, kv, half)

    def finish(kv):
        for half in range(2):
            for direction in range(2):
                origin = came_from(direction, 3)
                along(3, direction, 1, kv, half, origin).wait_recv()
                start_pair(origin, kv, half)
            origin = came_from(half, 4)
            along(4, half, 2, kv, half, origin).wait_recv()
            start_pair(origin, kv, half)

    def wait_pairs(kv):
        for origin in range(YN):
            for half in range(2):
                pair(origin, 1 - c, kv, half).wait_recv()

    values = vp.astype(BF16)
    keep(1, values)
    launch(1)
    turned = rotate(kp * kgain[...])
    keep(0, turned.astype(BF16))
    launch(0)
    q_sq, k_sq = total_squares(2, 0)
    q_scale = lax.rsqrt(q_sq / D + EPS)
    k_scale = lax.rsqrt(k_sq / D + EPS)
    ks_out[...] = jnp.where(lane[:ROWS] == 0, k_scale[:ROWS], 0.0).T[:8, :]
    new_rows(slot)[0] = (turned[ROWS:] * k_scale[ROWS:]).astype(BF16)
    new_rows(slot)[1] = values[ROWS:]
    queries = (rotate(qp * q_scale * qgain[...]) * QSCALE).astype(BF16)

    def send_scale(i, other):
        return remote(ks_out, ks_in.at[here], ks_ss.at[i], ks_rs.at[here],
                      seq=z * (YN * CN) + other)

    def start_scale(i, carry):
        send_scale(i, (here + i) % (YN * CN)).start()
        return carry

    lax.fori_loop(1, YN * CN, start_scale, 0)
    ks_in[here] = ks_out[...]
    forward(1)
    qcg[group] = queries[ROWS:]
    qg[z] = queries[:ROWS].reshape(2, BLK, W)

    pl.semaphore_wait(ready, 3)

    def cont_q(i, other):
        return remote(qcg.at[group], qcg.at[group], qc_ss.at[i], qc_rs.at[group],
                      seq=member(other))

    def start_cont_q(i, carry):
        cont_q(i, (group + i) % CGROUP).start()
        return carry

    lax.fori_loop(1, CGROUP, start_cont_q, 0)
    for i, seq in ((0, partner), (1, twin), (2, cross)):
        d = remote(new_rows(slot), new_rows(slot), new_ss.at[i], new_rs.at[slot], seq=seq)
        d.start()
        sends.append(d)

    for i in (2, 1, 3):
        go(remote(qg.at[z], qg.at[z], q_ss.at[i], q_rs.at[z], seq=seq_of((z + i) % ZN, y, c)))

    forward(0)
    remote(cache, cache_rows(twin_slot), cache_ss.at[0], cache_rs.at[twin_slot],
           seq=twin).wait_recv()
    d = remote(cache_rows(twin_slot), cache_rows(twin_slot), cache_ss.at[2],
               cache_rs.at[twin_slot], seq=partner)
    d.start()
    sends.append(d)
    loads[5].wait()
    for i, j in ((1, 2 * b + 1 - c), (2, 2 * (1 - b) + 1 - c)):
        remote(cache, cache_rows(j), cache_ss.at[i], cache_rs.at[j], seq=partner).wait_recv()
    for i, j in ((0, 2 * b + 1 - c), (1, twin_slot), (2, 2 * (1 - b) + 1 - c)):
        remote(new_rows(j), new_rows(j), new_ss.at[i], new_rs.at[j], seq=partner).wait_recv()

    def wait_cont_q(i, carry):
        other = (group + i) % CGROUP
        remote(qcg.at[other], qcg.at[other], qc_ss.at[i], qc_rs.at[other],
               seq=member(other)).wait_recv()
        return carry

    lax.fori_loop(1, CGROUP, wait_cont_q, 0)
    top = 2 * CN * YN * ZN - 1
    n = iota((1, CKEYS), 1)
    dead = 1 << 30
    j = n - QUAD * CAP
    key_dev = base + j // CROWS
    in_block = j % CROWS
    new_pos = jnp.where(
        in_block < CBLK,
        key_dev * CBLK + in_block,
        (top - key_dev) * CBLK + in_block - CBLK,
    )
    key_pos = jnp.where((n >= QUAD * CAP) & (n < pad0), new_pos, dead)
    for i in range(QUAD):
        live = (n >= i * CAP) & (n < i * CAP + lengths[base + i])
        key_pos = jnp.where(live, -1, key_pos)

    def cont_block(blk, carry):
        rq = blk * 128 + iota((128, 1), 0)
        who = rq // CROWS
        dev = seq_of(who // (YN // 2), (who % (YN // 2)) * 2 + b, c)
        off = rq % CROWS
        q_pos = jnp.where(off < CBLK, dev * CBLK + off, (top - dev) * CBLK + off - CBLK)
        allowed = key_pos <= q_pos
        q = qcg[pl.ds(blk * 8, 8)].reshape(128, W)
        parts = [
            attend(
                q[:, h * HD : (h + 1) * HD],
                kcc[0, :, h * HD : (h + 1) * HD],
                kcc[1, :, h * HD : (h + 1) * HD],
                allowed,
            )
            for h in range(2)
        ]
        oc_out[pl.ds(blk * 8, 8)] = message(parts).reshape(8, CROWS, MSG)
        return carry

    cont_block(0, 0)
    finish(1)
    cont_block(1, 0)

    def cont_o(i, other):
        return remote(oc_out.at[other], oc_in.at[group], oc_ss.at[i], oc_rs.at[group],
                      seq=member(other))

    def start_cont_o(i, carry):
        cont_o(i, (group + i) % CGROUP).start()
        return carry

    lax.fori_loop(1, CGROUP, start_cont_o, 0)

    ro = iota((128, 2 * KEYS), 0)
    co = iota((128, 2 * KEYS), 1)
    jj = ro % 16
    want = (ro // 32) * 16 + here
    pick_row = jnp.where(ro % 32 < 16, jj * BLK, KEYS + (15 - jj) * BLK) + want
    onehot = jnp.where(co == pick_row, 1.0, 0.0).astype(BF16)

    def cyclic_rows(kv):
        rows = jnp.dot(onehot, kvg[kv].reshape(2 * KEYS, W), preferred_element_type=F32)
        if kv == 0:
            rows = rows * jnp.sum(jnp.where(co == pick_row, key_scale, 0.0), -1, keepdims=True)
        kv_s[kv] = rows.astype(BF16).reshape(ZN, 2, 16, W)
        for i in (2, 1, 3):
            dst = (z + i) % ZN
            d = remote(kv_s.at[kv, dst], kv_r.at[kv, z], kv_ss.at[kv, i], kv_rs.at[kv, z],
                       seq=seq_of(dst, y, c))
            d.start()
            sends.append(d)

    finish(0)
    wait_pairs(1)
    cyclic_rows(1)
    for i in (2, 1, 3):
        src = (z + i) % ZN
        remote(qg.at[src], qg.at[src], q_ss.at[i], q_rs.at[src],
               seq=seq_of(src, y, c)).wait_recv()

    def wait_scale(i, carry):
        other = (here + i) % (YN * CN)
        remote(ks_out, ks_in.at[other], ks_ss.at[i], ks_rs.at[other],
               seq=z * (YN * CN) + other).wait_recv()
        return carry

    lax.fori_loop(1, YN * CN, wait_scale, 0)
    low_half = iota((8, 128), 1) < BLK
    lows, highs = [], []
    for i in range(YN):
        first, second = ks_in[2 * i], ks_in[2 * i + 1]
        lows.append(jnp.where(low_half, first, pltpu.roll(second, BLK, 1))[:1])
        highs.append(jnp.where(low_half, pltpu.roll(first, BLK, 1), second)[:1])
    key_scale = jnp.concatenate(lows + highs, 1)
    wait_pairs(0)

    n2 = iota((1, 2 * KEYS), 1)
    hi_n = n2 - KEYS
    key_pos2 = jnp.where(
        n2 < KEYS,
        z * KEYS + n2,
        (top - z * (YN * CN) - hi_n // BLK) * BLK + hi_n % BLK,
    )

    def prompt_block(i, carry):
        zq = (z + i) % ZN
        dev = zq * (YN * CN) + here
        rq = iota((ROWS, 1), 0)
        q_pos = jnp.where(rq < BLK, dev * BLK + rq, (top - dev) * BLK + rq - BLK)
        allowed = key_pos2 <= q_pos
        q = qg[zq].reshape(ROWS, W)
        parts = [
            attend(
                q[:, h * HD : (h + 1) * HD],
                kvg[0, :, :, h * HD : (h + 1) * HD].reshape(2 * KEYS, HD),
                kvg[1, :, :, h * HD : (h + 1) * HD].reshape(2 * KEYS, HD),
                allowed,
                key_scale,
            )
            for h in range(2)
        ]
        op_out[zq] = jnp.concatenate([p[0].astype(BF16) for p in parts], -1).reshape(2, BLK, W)
        stats = jnp.zeros((ROWS, 128), F32)
        for h in range(2):
            stats = jnp.where(lane[:ROWS] == 2 * h, parts[h][1], stats)
            stats = jnp.where(lane[:ROWS] == 2 * h + 1, parts[h][2], stats)
        os_out[zq] = stats.T[:8, :]
        return carry

    def stats_o(i, dst):
        return remote(os_out.at[dst], os_in.at[z], os_ss.at[i], os_rs.at[z],
                      seq=seq_of(dst, y, c))

    def near_o(i, dst):
        return remote(op_out.at[dst], op_in.at[z], op_ss.at[i], op_rs.at[z],
                      seq=seq_of(dst, y, c))

    for i in (2, 1, 3):
        prompt_block(i, 0)
        dst = (z + i) % ZN
        go(near_o(i, dst), stats_o(i, dst))
    prompt_block(0, 0)
    cyclic_rows(0)

    def wait_cont_o(i, carry):
        other = (group + i) % CGROUP
        remote(oc_out.at[other], oc_in.at[other], oc_ss.at[i], oc_rs.at[other],
               seq=member(other)).wait_recv()
        return carry

    lax.fori_loop(1, CGROUP, wait_cont_o, 0)
    oc_in[group] = oc_out[group]
    cont_parts = [oc_in[i] for i in range(CGROUP)]
    att[ROWS:, :] = combine(cont_parts, [message_stats(p) for p in cont_parts])
    pieces, stats = [op_out[z].reshape(ROWS, W)], [os_out[z]]
    for i in (1, 3, 2):
        src = (z + i) % ZN
        remote(op_out.at[src], op_in.at[src], op_ss.at[i], op_rs.at[src],
               seq=seq_of(src, y, c)).wait_recv()
        remote(os_out.at[src], os_in.at[src], os_ss.at[i], os_rs.at[src],
               seq=seq_of(src, y, c)).wait_recv()
        pieces.append(op_in[src].reshape(ROWS, W))
        stats.append(os_in[src])
    cols = jnp.concatenate(stats + [jnp.zeros((96, 128), F32)], 0).T
    att[:ROWS, :] = combine(
        pieces,
        [
            [
                (cols[:, 8 * i + 2 * h : 8 * i + 2 * h + 1],
                 cols[:, 8 * i + 2 * h + 1 : 8 * i + 2 * h + 2])
                for h in range(2)
            ]
            for i in range(ZN)
        ],
    )

    for load in loads[6:]:
        load.wait()
    a = att[...]

    def project(p):
        return jnp.dot(a, wo[p], preferred_element_type=F32).astype(BF16)

    for i in (6, 5, 4, 3, 2, 1, 0):
        p = peers[i]
        pr_out[p] = project(p)
        go(remote(pr_out.at[p], pr_in.at[t], pr_ss.at[i], pr_rs.at[t], tp=p))
    proj = project(t).astype(F32)
    for i in range(7):
        p = peers[i]
        remote(pr_out.at[p], pr_in.at[p], pr_ss.at[i], pr_rs.at[p], tp=p).wait_recv()
        proj = proj + pr_in[p].astype(F32)

    send_squares([jnp.sum(proj * proj, -1, keepdims=True)], 1)
    (p_sq,) = total_squares(1, 1)
    normed = proj * lax.rsqrt(p_sq / D + EPS) * pgain[...]
    hid_p[...] = (xg[t].astype(F32) + normed[:ROWS].reshape(2, BLK, W)).astype(BF16)
    hid_c[...] = (xc[t].astype(F32) + normed[ROWS:].reshape(2, CBLK, W)).astype(BF16)

    for kv in range(2):
        for i in (1, 3, 2):
            src = (z + i) % ZN
            remote(kv_s.at[kv, src], kv_r.at[kv, src], kv_ss.at[kv, i], kv_rs.at[kv, src],
                   seq=seq_of(src, y, c)).wait_recv()
        kv_r[kv, z] = kv_s[kv, z]
        for src in range(ZN):
            kv_out[kv, 16 * src : 16 * src + 16, :] = kv_r[kv, src, 0]
            kv_out[kv, 112 - 16 * src : 128 - 16 * src, :] = kv_r[kv, src, 1]

    for d in sends:
        d.wait_send()

    def drain(i, carry):
        cont_q(i, (group + i) % CGROUP).wait_send()
        cont_o(i, (group + i) % CGROUP).wait_send()
        send_scale(i, (here + i) % (YN * CN)).wait_send()
        return carry

    lax.fori_loop(1, CGROUP, drain, 0)


def per_device(
    prompt_states, cont_states, cache_kv, cache_lengths, w_query, w_key, w_value, w_out,
    q_gain, k_gain, post_gain,
):
    half = HD // 2
    freq = THETA ** (-(np.arange(half) * 2.0 / HD))
    inv = jnp.asarray(np.concatenate([freq, freq])[None, :].astype(np.float32))
    any_ = pl.BlockSpec(memory_space=pl.ANY)
    vmem = pl.BlockSpec(memory_space=pltpu.VMEM)
    smem = pl.BlockSpec(memory_space=pltpu.SMEM)
    dma = pltpu.SemaphoreType.DMA
    hid_p, hid_c, kv = pl.pallas_call(
        kernel,
        out_shape=(
            jax.ShapeDtypeStruct((2, BLK, W), BF16),
            jax.ShapeDtypeStruct((2, CBLK, W), BF16),
            jax.ShapeDtypeStruct((2, 2 * BLK, W), BF16),
        ),
        in_specs=[any_, any_, any_, smem, any_, any_, any_, any_, vmem, vmem, vmem, vmem],
        out_specs=(vmem, vmem, vmem),
        scratch_shapes=[
            pltpu.VMEM((D, W), BF16),
            pltpu.VMEM((D, W), BF16),
            pltpu.VMEM((D, W), BF16),
            pltpu.VMEM((TP, W, W), BF16),
            pltpu.VMEM((TP, 2, BLK, W), BF16),
            pltpu.VMEM((TP, 2, CBLK, W), BF16),
            pltpu.VMEM((ALL, 128), F32),
            pltpu.VMEM((ALL, 128), F32),
            pltpu.VMEM((2, 8, 256), F32),
            pltpu.VMEM((2, TP, 8, 256), F32),
            pltpu.VMEM((ZN, 2, BLK, W), BF16),
            pltpu.VMEM((2, 2, KEYS, W), BF16),
            pltpu.VMEM((CGROUP, CROWS, W), BF16),
            pltpu.VMEM((2, CKEYS, W), BF16),
            pltpu.VMEM((CGROUP, CROWS, MSG), BF16),
            pltpu.VMEM((CGROUP, CROWS, MSG), BF16),
            pltpu.VMEM((ZN, 2, BLK, W), BF16),
            pltpu.VMEM((ZN, 2, BLK, W), BF16),
            pltpu.VMEM((ZN, 8, 128), F32),
            pltpu.VMEM((ZN, 8, 128), F32),
            pltpu.VMEM((2, ZN, 2, 16, W), BF16),
            pltpu.VMEM((2, ZN, 2, 16, W), BF16),
            pltpu.VMEM((ALL, W), BF16),
            pltpu.VMEM((TP, ALL, W), BF16),
            pltpu.VMEM((TP, ALL, W), BF16),
            pltpu.VMEM((8, 128), F32),
            pltpu.VMEM((YN * CN, 8, 128), F32),
            dma((6 + TP,)),
            dma((7,)), dma((TP,)), dma((7,)), dma((TP,)),
            dma((2, 7)), dma((2, TP)),
            dma((3,)), dma((QUAD,)), dma((3,)), dma((QUAD,)),
            pltpu.SemaphoreType.REGULAR,
            dma((CGROUP,)), dma((CGROUP,)),
            dma((ZN,)), dma((ZN,)),
            dma((2, 5, 2, 2)), dma((2, 5, 2, 2)),
            dma((YN, 2, 2)), dma((YN, 2, 2)),
            dma((CGROUP,)), dma((CGROUP,)),
            dma((ZN,)), dma((ZN,)), dma((ZN,)), dma((ZN,)),
            dma((2, ZN)), dma((2, ZN)),
            dma((7,)), dma((TP,)),
            dma((YN * CN,)), dma((YN * CN,)),
        ],
        compiler_params=pltpu.CompilerParams(
            collective_id=0, has_side_effects=True, vmem_limit_bytes=60 * 1024 * 1024
        ),
        name="block",
    )(
        prompt_states[:, 0], cont_states[:, 0], cache_kv[:, 0], cache_lengths,
        w_query, w_key, w_value, w_out,
        q_gain[None], k_gain[None], post_gain[None], inv,
    )
    return hid_p[:, None], hid_c[:, None], kv[:, None]


def solution(mesh):
    return jax.shard_map(
        per_device,
        mesh=mesh,
        in_specs=(
            P(None, "seq", None, "tp"),
            P(None, "seq", None, "tp"),
            P(None, "seq", None, "tp"),
            P(),
            P(None, "tp"),
            P(None, "tp"),
            P(None, "tp"),
            P("tp", None),
            P("tp"),
            P("tp"),
            P("tp"),
        ),
        out_specs=(
            P(None, "seq", None, "tp"),
            P(None, "seq", None, "tp"),
            P(None, "seq", None, "tp"),
        ),
        check_vma=False,
    )
```

time: 92.3 us -> 87.2 us (0.945)
  Pallas kernels: 88.7 us -> 83.6 us
    pallas_call x1, Pallas kernels: 88.7 us -> 83.6 us  [per_device(): pl.pallas_call(kernel, out_shape=(jax.ShapeDtypeStruct((2, BLK, W), BF16)...]
where the time goes in v2:
time: 87.2 us; the launch traced here: 87 us
  Pallas kernels  83.6 us (96%)
  local copies, waits for them, and re-layouts  2.78 us (3%)
    pallas_call x1, Pallas kernels, per_device(): pl.pallas_call(kernel, out_shape=(jax.ShapeDtypeStruct((2, BLK, W), BF16)...  83.6 us
    unnamed x7, local copies, waits for them, and re-layouts  2.78 us

profile of v2, /device:TPU:1, one launch (start us, length us, event | category | flops | bytes accessed | tf_op | source)
XLA Modules:
  0.0 87.0 jit_solution(4059992945982298332)
XLA Ops:
  0.6 83.6 %block.1 = (bf16[2,64,256]{2,1,0:T(8,128)(2,1)}, bf16[2,8,256]{2,1,0:T(8,128)(2,1)}, bf16[2,128,256]{2,1,0:T(8,128)(2,1)}) custom-call(bf16[2,64,256]{2,1,0:T(8,128)(2,1)} %bitcast.17, bf16[2,8,256]{2,1,0:T(8,128)(2,1)} %bitcast.19, bf16[2,448,256]{2,1,0:T(8,128)(2,1)} %bitcast.15, s32[64]{0:T(128)} %lengths.1, bf16[2048,256]{1,0:T(8,128)(2,1)} %wq_h.1, ...), custom_call_target="tpu_custom_call" | custom-call | tf_op jit(solution)/shard_map/block/pallas_call | solution.py:622
  84.2 0.0 copy-start
  84.2 0.0 copy-start.1
  84.2 1.5 %copy.21 = bf16[2,1,64,256]{3,2,1,0:T(8,128)(2,1)} copy(bf16[2,1,64,256]{3,2,1,0:T(8,128)(2,1)} %bitcast.18) | data formatting | bytes 131072
  85.7 0.0 copy-done.1
  85.7 0.6 copy.22
  86.3 0.0 copy-done
  86.3 0.7 copy.23
Async XLA Ops:
  84.2 2.1 %copy-start = (bf16[2,128,256]{2,1,0:T(8,128)(2,1)S(1)}, bf16[2,128,256]{2,1,0:T(8,128)(2,1)}, u32[]{:S(2)}) copy-start(bf16[2,128,256]{2,1,0:T(8,128)(2,1)} %get-tuple-element.8) | copy-start | bytes 393220
  84.2 1.5 %copy-start.1 = (bf16[2,8,256]{2,1,0:T(8,128)(2,1)S(1)}, bf16[2,8,256]{2,1,0:T(8,128)(2,1)}, u32[]{:S(2)}) copy-start(bf16[2,8,256]{2,1,0:T(8,128)(2,1)} %get-tuple-element.7) | copy-start | bytes 24580

commit v3 on v2

--- a/solution.py
+++ b/solution.py
@@ -84,11 +84,11 @@
     hid_p, hid_c, kv_out,
     wq, wk, wv, wo, xg, xc, cos, sin, sq_out, sq_in, qg, kvg, qcg, kcc,
     oc_out, oc_in, op_out, op_in, os_out, os_in, kv_s, kv_r, att, pr_out, pr_in,
-    ks_out, ks_in,
-    local, tp_ss, tp_rs, tpc_ss, tpc_rs, sq_ss, sq_rs, cache_ss, cache_rs, new_ss, new_rs, ready,
+    ks_out, ks_in, zr_lo, zr_hi,
+    local, tp_ss, tp_rs, tpf_ss, sq_ss, sq_rs, cache_ss, cache_rs, new_ss, new_rs, ready,
     qc_ss, qc_rs, q_ss, q_rs, ring_ss, ring_rs, pair_ss, pair_rs,
     oc_ss, oc_rs, op_ss, op_rs, os_ss, os_rs, kv_ss, kv_rs, pr_ss, pr_rs,
-    ks_ss, ks_rs,
+    ks_ss, ks_rs, qf_ss, zr_ss, zr_rs, zf_ss, zf_rs,
 ):
     s_idx = lax.axis_index("seq")
     t = lax.axis_index("tp")
@@ -160,19 +160,20 @@
         signal(ready, seq_of((z + i) % ZN, y, c), t)
 
     sends = []
-    def go(*copies):
-        for d in copies:
+    def row_part(i, part, origin, to):
+        if origin is None:
+            src, origin = (cont if part == 2 else prompt.at[part]), t
+        else:
+            src = xc.at[origin] if part == 2 else xg.at[origin, part]
+        dst = xc.at[origin] if part == 2 else xg.at[origin, part]
+        ss = tp_ss.at[i, part] if i < 5 else tpf_ss.at[i - 5, part]
+        return remote(src, dst, ss, tp_rs.at[origin, part], tp=to)
+
+    for part in range(3):
+        for i in (1, 2, 3, 4, 0):
+            d = row_part(i, part, None, peers[i])
             d.start()
             sends.append(d)
-
-    def rows_to(i):
-        return remote(prompt, xg.at[t], tp_ss.at[i], tp_rs.at[t], tp=peers[i])
-
-    def new_to(i):
-        return remote(cont, xc.at[t], tpc_ss.at[i], tpc_rs.at[t], tp=peers[i])
-
-    for i in (6, 5, 4, 3, 2, 1, 0):
-        go(rows_to(i), new_to(i))
     for i, seq in ((0, twin), (1, partner)):
         d = remote(cache, cache_rows(slot), cache_ss.at[i], cache_rs.at[slot], seq=seq)
         d.start()
@@ -198,13 +199,19 @@
     qp = jnp.zeros((ALL, W), F32)
     kp = jnp.zeros((ALL, W), F32)
     vp = jnp.zeros((ALL, W), F32)
-    for i in range(-1, 7):
+    for i in (-1, 2, 1, 0, 4, 3, 5, 6):
         if i < 0:
             src = t
         else:
             src = peers[i]
-            remote(prompt, xg.at[src], tp_ss.at[i], tp_rs.at[src], tp=src).wait_recv()
-            remote(cont, xc.at[src], tpc_ss.at[i], tpc_rs.at[src], tp=src).wait_recv()
+            for part in range(3):
+                row_part(0, part, src, src).wait_recv()
+                if (i == 2 and part != 1) or (i == 1 and part == 1):
+                    for to in range(2):
+                        near = ((x + 1) % 4 if i == 2 else (x + 3) % 4) * 2 + to
+                        d = row_part(5 + to, part, src, near)
+                        d.start()
+                        sends.append(d)
         rows = jnp.concatenate(
             [
                 xg[src].reshape(ROWS, W),
@@ -263,12 +270,13 @@
         rows = pl.ds(pl.multiple_of((2 * origin_y + core) * BLK, BLK), BLK)
         return kvg.at[kv, half, rows, :]
 
-    def along(hop, direction, dist, kv, half, origin):
-        step = dist if direction == 0 else YN - dist
+    right, left = seq_of(z, (y + 1) % YN, c), seq_of(z, (y + YN - 1) % YN, c)
+
+    def ring(direction, step, kv, half, origin):
         return remote(
             piece(origin, c, kv, half), piece(origin, c, kv, half),
-            ring_ss.at[direction, hop, kv, half], ring_rs.at[direction, hop, kv, half],
-            seq=seq_of(z, (y + step) % YN, c),
+            ring_ss.at[direction, step, kv, half], ring_rs.at[direction, step, kv, half],
+            seq=right if direction == 0 else left,
         )
 
     def pair(origin, core, kv, half):
@@ -282,41 +290,24 @@
         d.start()
         sends.append(d)
 
-    def launch(kv):
-        for dist in (2, 1):
-            for half in range(2):
-                for direction in range(2):
-                    go(along(dist, direction, dist, kv, half, y))
-        for half in range(2):
-            start_pair(y, kv, half)
-
-    def came_from(direction, dist):
-        return (y + (YN - dist if direction == 0 else dist)) % YN
-
-    def forward(kv):
+    def launch(step, kv):
         for half in range(2):
             for direction in range(2):
-                origin = came_from(direction, 2)
-                along(2, direction, 2, kv, half, origin).wait_recv()
-                if direction == half:
-                    go(along(4, direction, 2, kv, half, origin))
-                go(along(3, direction, 1, kv, half, origin))
-                start_pair(origin, kv, half)
-        for half in range(2):
-            for direction in range(2):
-                origin = came_from(direction, 1)
-                along(1, direction, 1, kv, half, origin).wait_recv()
-                start_pair(origin, kv, half)
+                origin = (y + (YN - step + 1 if direction == 0 else step - 1)) % YN
+                if step > 1:
+                    ring(direction, step - 1, kv, half, origin).wait_recv()
+                if step < 4 or direction == half:
+                    d = ring(direction, step, kv, half, origin)
+                    d.start()
+                    sends.append(d)
+                if step > 1 or direction == 0:
+                    start_pair(origin, kv, half)
 
     def finish(kv):
         for half in range(2):
-            for direction in range(2):
-                origin = came_from(direction, 3)
-                along(3, direction, 1, kv, half, origin).wait_recv()
-                start_pair(origin, kv, half)
-            origin = came_from(half, 4)
-            along(4, half, 2, kv, half, origin).wait_recv()
-            start_pair(origin, kv, half)
+            far = (y + 4) % YN
+            ring(half, 4, kv, half, far).wait_recv()
+            start_pair(far, kv, half)
 
     def wait_pairs(kv):
         for origin in range(YN):
@@ -325,10 +316,11 @@
 
     values = vp.astype(BF16)
     keep(1, values)
-    launch(1)
+    launch(1, 1)
     turned = rotate(kp * kgain[...])
     keep(0, turned.astype(BF16))
-    launch(0)
+    launch(1, 0)
+    launch(2, 1)
     q_sq, k_sq = total_squares(2, 0)
     q_scale = lax.rsqrt(q_sq / D + EPS)
     k_scale = lax.rsqrt(k_sq / D + EPS)
@@ -347,7 +339,7 @@
 
     lax.fori_loop(1, YN * CN, start_scale, 0)
     ks_in[here] = ks_out[...]
-    forward(1)
+    launch(2, 0)
     qcg[group] = queries[ROWS:]
     qg[z] = queries[:ROWS].reshape(2, BLK, W)
 
@@ -367,16 +359,34 @@
         d.start()
         sends.append(d)
 
-    for i in (2, 1, 3):
-        go(remote(qg.at[z], qg.at[z], q_ss.at[i], q_rs.at[z], seq=seq_of((z + i) % ZN, y, c)))
-
-    forward(0)
+    def prompt_q(i, half, origin, dst):
+        ss = q_ss.at[i, half] if i < 2 else qf_ss.at[half]
+        return remote(qg.at[origin, half], qg.at[origin, half], ss, q_rs.at[origin, half],
+                      seq=seq_of(dst, y, c))
+
+    up, down, over = (z + 1) % ZN, (z + 3) % ZN, (z + 2) % ZN
+    for half in range(2):
+        for i, dst in ((0, up), (1, down)):
+            d = prompt_q(i, half, z, dst)
+            d.start()
+            sends.append(d)
+
+    launch(3, 1)
     remote(cache, cache_rows(twin_slot), cache_ss.at[0], cache_rs.at[twin_slot],
            seq=twin).wait_recv()
     d = remote(cache_rows(twin_slot), cache_rows(twin_slot), cache_ss.at[2],
                cache_rs.at[twin_slot], seq=partner)
     d.start()
     sends.append(d)
+    launch(3, 0)
+    launch(4, 1)
+    launch(4, 0)
+    for half, origin, dst in ((0, down, up), (1, up, down)):
+        prompt_q(0, half, origin, dst).wait_recv()
+        d = prompt_q(2, half, origin, dst)
+        d.start()
+        sends.append(d)
+
     loads[5].wait()
     for i, j in ((1, 2 * b + 1 - c), (2, 2 * (1 - b) + 1 - c)):
         remote(cache, cache_rows(j), cache_ss.at[i], cache_rs.at[j], seq=partner).wait_recv()
@@ -461,11 +471,8 @@
 
     finish(0)
     wait_pairs(1)
-    cyclic_rows(1)
-    for i in (2, 1, 3):
-        src = (z + i) % ZN
-        remote(qg.at[src], qg.at[src], q_ss.at[i], q_rs.at[src],
-               seq=seq_of(src, y, c)).wait_recv()
+    for half, origin in ((1, down), (0, up), (0, over), (1, over)):
+        prompt_q(0, half, origin, origin).wait_recv()
 
     def wait_scale(i, carry):
         other = (here + i) % (YN * CN)
@@ -524,12 +531,30 @@
         return remote(op_out.at[dst], op_in.at[z], op_ss.at[i], op_rs.at[z],
                       seq=seq_of(dst, y, c))
 
-    for i in (2, 1, 3):
-        prompt_block(i, 0)
-        dst = (z + i) % ZN
-        go(near_o(i, dst), stats_o(i, dst))
+    def far_o(half, dst):
+        return remote(op_out.at[over, half], zr_lo if half == 0 else zr_hi, zr_ss.at[half],
+                      zr_rs.at[half], seq=seq_of(dst, y, c))
+
+    def pass_o(half, origin, dst):
+        return remote(zr_lo if half == 0 else zr_hi, op_in.at[origin, half], zf_ss.at[half],
+                      zf_rs.at[half], seq=seq_of(dst, y, c))
+
+    def go(*copies):
+        for d in copies:
+            d.start()
+            sends.append(d)
+
+    prompt_block(2, 0)
+    go(far_o(0, up), far_o(1, down), stats_o(2, over))
+    prompt_block(1, 0)
+    go(near_o(1, up), stats_o(1, up))
+    prompt_block(3, 0)
+    go(near_o(3, down), stats_o(3, down))
+    far_o(0, up).wait_recv()
+    go(pass_o(0, down, up))
+    far_o(1, down).wait_recv()
+    go(pass_o(1, up, down))
     prompt_block(0, 0)
-    cyclic_rows(0)
 
     def wait_cont_o(i, carry):
         other = (group + i) % CGROUP
@@ -544,8 +569,12 @@
     pieces, stats = [op_out[z].reshape(ROWS, W)], [os_out[z]]
     for i in (1, 3, 2):
         src = (z + i) % ZN
-        remote(op_out.at[src], op_in.at[src], op_ss.at[i], op_rs.at[src],
-               seq=seq_of(src, y, c)).wait_recv()
+        if i == 2:
+            pass_o(0, src, z).wait_recv()
+            pass_o(1, src, z).wait_recv()
+        else:
+            remote(op_out.at[src], op_in.at[src], op_ss.at[i], op_rs.at[src],
+                   seq=seq_of(src, y, c)).wait_recv()
         remote(os_out.at[src], os_in.at[src], os_ss.at[i], os_rs.at[src],
                seq=seq_of(src, y, c)).wait_recv()
         pieces.append(op_in[src].reshape(ROWS, W))
@@ -574,6 +603,8 @@
         p = peers[i]
         pr_out[p] = project(p)
         go(remote(pr_out.at[p], pr_in.at[t], pr_ss.at[i], pr_rs.at[t], tp=p))
+    cyclic_rows(1)
+    cyclic_rows(0)
     proj = project(t).astype(F32)
     for i in range(7):
         p = peers[i]
@@ -656,20 +687,23 @@
             pltpu.VMEM((TP, ALL, W), BF16),
             pltpu.VMEM((8, 128), F32),
             pltpu.VMEM((YN * CN, 8, 128), F32),
+            pltpu.VMEM((BLK, W), BF16),
+            pltpu.VMEM((BLK, W), BF16),
             dma((6 + TP,)),
-            dma((7,)), dma((TP,)), dma((7,)), dma((TP,)),
+            dma((5, 3)), dma((TP, 3)), dma((2, 3)),
             dma((2, 7)), dma((2, TP)),
             dma((3,)), dma((QUAD,)), dma((3,)), dma((QUAD,)),
             pltpu.SemaphoreType.REGULAR,
             dma((CGROUP,)), dma((CGROUP,)),
-            dma((ZN,)), dma((ZN,)),
+            dma((2, 2)), dma((ZN, 2)),
             dma((2, 5, 2, 2)), dma((2, 5, 2, 2)),
             dma((YN, 2, 2)), dma((YN, 2, 2)),
             dma((CGROUP,)), dma((CGROUP,)),
             dma((ZN,)), dma((ZN,)), dma((ZN,)), dma((ZN,)),
             dma((2, ZN)), dma((2, ZN)),
             dma((7,)), dma((TP,)),
-            dma((YN * CN,)), dma((YN * CN,)),
+            dma((YN * CN,)), dma((YN * CN,)), dma((2,)),
+            dma((2,)), dma((2,)), dma((2,)), dma((2,)),
         ],
         compiler_params=pltpu.CompilerParams(
             collective_id=0, has_side_effects=True, vmem_limit_bytes=60 * 1024 * 1024

time: 87.2 us -> 80.4 us (0.922); the launches traced: 87 us -> 79.3 us
  Pallas kernels: 83.6 us -> 75.9 us
    pallas_call x1, Pallas kernels: 83.6 us -> 75.9 us  [per_device(): pl.pallas_call(kernel, out_shape=(jax.ShapeDtypeStruct((2, BLK, W), BF16)...]
where the time goes in v3:
time: 80.4 us; the launch traced here: 79.3 us
  Pallas kernels  75.9 us (94%)
  local copies, waits for them, and re-layouts  2.78 us (3%)
    pallas_call x1, Pallas kernels, per_device(): pl.pallas_call(kernel, out_shape=(jax.ShapeDtypeStruct((2, BLK, W), BF16)...  75.9 us
    unnamed x7, local copies, waits for them, and re-layouts  2.78 us

profile of v3, /device:TPU:1, one launch (start us, length us, event | category | flops | bytes accessed | tf_op | source)
XLA Modules:
  0.0 79.3 jit_solution(9902531905410417627)
XLA Ops:
  0.6 75.9 %block.1 = (bf16[2,64,256]{2,1,0:T(8,128)(2,1)}, bf16[2,8,256]{2,1,0:T(8,128)(2,1)}, bf16[2,128,256]{2,1,0:T(8,128)(2,1)}) custom-call(bf16[2,64,256]{2,1,0:T(8,128)(2,1)} %bitcast.17, bf16[2,8,256]{2,1,0:T(8,128)(2,1)} %bitcast.19, bf16[2,448,256]{2,1,0:T(8,128)(2,1)} %bitcast.15, s32[64]{0:T(128)} %lengths.1, bf16[2048,256]{1,0:T(8,128)(2,1)} %wq_h.1, ...), custom_call_target="tpu_custom_call" | custom-call | tf_op jit(solution)/shard_map/block/pallas_call | solution.py:653
  76.5 0.0 copy-start
  76.5 0.0 copy-start.1
  76.5 1.5 %copy.21 = bf16[2,1,64,256]{3,2,1,0:T(8,128)(2,1)} copy(bf16[2,1,64,256]{3,2,1,0:T(8,128)(2,1)} %bitcast.18) | data formatting | bytes 131072
  78.1 0.0 copy-done.1
  78.1 0.6 copy.22
  78.7 0.0 copy-done
  78.7 0.7 copy.23
Async XLA Ops:
  76.5 2.1 %copy-start = (bf16[2,128,256]{2,1,0:T(8,128)(2,1)S(1)}, bf16[2,128,256]{2,1,0:T(8,128)(2,1)}, u32[]{:S(2)}) copy-start(bf16[2,128,256]{2,1,0:T(8,128)(2,1)} %get-tuple-element.8) | copy-start | bytes 393220
  76.5 1.5 %copy-start.1 = (bf16[2,8,256]{2,1,0:T(8,128)(2,1)S(1)}, bf16[2,8,256]{2,1,0:T(8,128)(2,1)}, u32[]{:S(2)}) copy-start(bf16[2,8,256]{2,1,0:T(8,128)(2,1)} %get-tuple-element.7) | copy-start | bytes 24580
